TPU v7x, 256 devices: a whole 4x4x8 slice. The times are simulated.
256 devices in a mesh: dp: 8 (over x, core), ctx: 32 (over y, z).
Axes of the slice: x: 4, y: 4, z: 8, core: 2. Of those that a mesh axis runs over, the one named last changes fastest.
Arguments:
- merged_grad: bfloat16 [32768, 1792], P(('dp', 'ctx')), may hold values from -6 to 6
- merged_owner: int32 [32768, 1], P(('dp', 'ctx')), may hold values from 0 to 31; in each aligned block of 128 rows (0 to 127, 128 to 255, ...) at most 8 rows name the same one
- merger_pre: bfloat16 [65536, 2560], P(('dp', 'ctx')), may hold values from -24 to 24
- fc2_weight: bfloat16 [2560, 1792], P('ctx'), may hold values from -0.125 to 0.125
- query: bfloat16 [65536, 1280], P(('dp', 'ctx')), may hold values from -32 to 32
- key_states: bfloat16 [65536, 1280], P(('dp', 'ctx')), may hold values from -32 to 32
- value_states: bfloat16 [65536, 1280], P(('dp', 'ctx')), may hold values from -6 to 6
- out_grad: bfloat16 [65536, 1280], P(('dp', 'ctx')), may hold values from -6 to 6
- position: int32 [2, 65536], P(None, ('dp', 'ctx')), may hold values from 0 to 63, as said below
Outputs:
- hidden_grad: bfloat16 [65536, 2560], P(('dp', 'ctx'))
- weight_grad: float32 [2560, 1792], P('ctx', 'dp')
- query_grad: bfloat16 [65536, 1280], P(('dp', 'ctx'))
- key_grad: bfloat16 [65536, 1280], P(('dp', 'ctx'))
- value_grad: bfloat16 [65536, 1280], P(('dp', 'ctx'))
Inputs may be any that keep to these rules, and one draw needn't show every extreme that they name: `merged_owner`: in each device's block of 128 rows no owner is named more than 8 times. `position`: each window of 64 consecutive patches covers an aligned square of 8 by 8 grid positions, row by row.
All inputs are finite; a program needn't handle non-finite values.
Results may differ from a plain program's by a relative error of at most 0.0017.
The roundings to bfloat16 on the way count: a program that leaves them out, or rounds other values in their place, can miss the bound.
Values may be sent and summed in bfloat16 or wider, within the bound.
No kernel may reach another device: no remote copies, remote signals or barrier semaphores. Data moves between devices by JAX's collectives and lax.ppermute only.
A program may use at most 128 MiB of HBM per device.

v0:
```python
import math

import jax
import jax.numpy as jnp
from jax import lax
from jax.sharding import Mesh
from jax.sharding import PartitionSpec as P

D = 1280
HEADS = 16
HEAD = 80
WIN = 64
CTX = ("ctx_0", "ctx_1")
DP_CTX = ("dp", "ctx_0", "ctx_1")


def sent_to_all(x, axis):
    copies = jnp.broadcast_to(x, (lax.axis_size(axis), *x.shape))
    return lax.all_to_all(copies, axis, split_axis=0, concat_axis=0, tiled=True)


def combined_pairwise(pieces, combine):
    while len(jax.tree.leaves(pieces)[0]) > 1:
        pieces = jax.vmap(combine)(*(pieces[side::2] for side in (0, 1)))
    return pieces[0]


def entering(x, axis, combine, identity):
    peers, place = (lax.axis_size(axis), lax.axis_index(axis))
    passed = jnp.arange(peers) < place

    def kept(part, zero, own):
        part = jnp.where(
            passed.reshape(-1, *(1 for _ in own.shape)), part, jnp.asarray(zero, own.dtype)
        )
        return part

    pieces = sent_to_all(x, axis)
    return combined_pairwise(kept(pieces, identity, x), combine)


def sum_by_axis(x, axes, dim):
    if not axes:
        return x
    nearer = lax.psum_scatter(x, axes[0], scatter_dimension=dim, tiled=True)
    return sum_by_axis(nearer, axes[1:], dim)


def rope_angles(position, head_size):
    quarter = head_size // 4
    freq = 1.0 / 10000.0 ** (jnp.arange(quarter, dtype=jnp.float32) * (4.0 / head_size))
    rows = position[0].astype(jnp.float32)[:, None] * freq[None, :]
    cols = position[1].astype(jnp.float32)[:, None] * freq[None, :]
    return jnp.concatenate([rows, cols], axis=1)


def rotate(values, angles, sign):
    half = values.shape[-1] // 2
    cosine = jnp.cos(angles)[:, None, :]
    sine = sign * jnp.sin(angles)[:, None, :]
    first = values[..., :half]
    second = values[..., half:]
    return jnp.concatenate(
        [first * cosine - second * sine, second * cosine + first * sine], axis=-1
    )


def attention_block(query, key_states, value_states, out_grad, position):
    count = query.shape[0]
    windows = count // WIN
    angles = rope_angles(position, HEAD)
    shaped = (count, HEADS, HEAD)
    grouped = (windows, WIN, HEADS, HEAD)
    q_rot = (
        rotate(query.astype(jnp.float32).reshape(shaped), angles, 1.0)
        .astype(jnp.bfloat16)
        .reshape(grouped)
    )
    k_rot = (
        rotate(key_states.astype(jnp.float32).reshape(shaped), angles, 1.0)
        .astype(jnp.bfloat16)
        .reshape(grouped)
    )
    v_win = value_states.reshape(grouped)
    g_win = out_grad.reshape(grouped)
    factor = HEAD ** (-0.5)
    f32 = jnp.float32
    scores = jnp.einsum("wqhd,wkhd->whqk", q_rot, k_rot, preferred_element_type=f32) * factor
    probs = jax.nn.softmax(scores, axis=-1)
    probs_b = probs.astype(jnp.bfloat16)
    output = jnp.einsum("whqk,wkhd->wqhd", probs_b, v_win, preferred_element_type=f32)
    value_grad = jnp.einsum("whqk,wqhd->wkhd", probs_b, g_win, preferred_element_type=f32).astype(
        jnp.bfloat16
    )
    prob_grad = jnp.einsum("wqhd,wkhd->whqk", g_win, v_win, preferred_element_type=f32)
    delta = jnp.transpose(jnp.sum(g_win.astype(f32) * output, axis=-1), (0, 2, 1))[..., None]
    score_grad = (probs * (prob_grad - delta)).astype(jnp.bfloat16)
    q_grad = jnp.einsum("whqk,wkhd->wqhd", score_grad, k_rot, preferred_element_type=f32) * factor
    k_grad = jnp.einsum("whqk,wqhd->wkhd", score_grad, q_rot, preferred_element_type=f32) * factor
    query_grad = rotate(q_grad.reshape(shaped), angles, -1.0).astype(jnp.bfloat16).reshape(count, D)
    key_grad = rotate(k_grad.reshape(shaped), angles, -1.0).astype(jnp.bfloat16).reshape(count, D)
    return (query_grad, key_grad, value_grad.reshape(count, D))


def add_counts(earlier, later):
    return earlier + later


def shards(
    merged_grad,
    merged_owner,
    merger_pre,
    fc2_weight,
    query,
    key_states,
    value_states,
    out_grad,
    position,
):
    rows_here = merged_grad.shape[0]
    owners_count = lax.axis_size(CTX)
    replicas = lax.axis_size("dp")
    slots = merger_pre.shape[0]
    capacity = slots // owners_count
    owner = merged_owner[:, 0]
    peers = jnp.arange(owners_count, dtype=jnp.int32)
    onehot = (owner[:, None] == peers[None, :]).astype(jnp.int32)
    counts = jnp.sum(onehot, axis=0, dtype=jnp.int32)
    running = jnp.cumsum(onehot, axis=0, dtype=jnp.int32)
    local_rank = jnp.sum(running * onehot, axis=1, dtype=jnp.int32) - 1
    before = entering(counts, CTX, add_counts, jnp.zeros_like(counts))
    slot_of_row = jnp.sum(onehot * before[None, :], axis=1, dtype=jnp.int32) + local_rank
    target = owner * capacity + local_rank
    places = jnp.arange(owners_count * capacity, dtype=jnp.int32)
    select = places[:, None] == target[None, :]
    outgoing = jnp.dot(select.astype(jnp.bfloat16), merged_grad, preferred_element_type=jnp.float32)
    outgoing = outgoing.astype(jnp.bfloat16).reshape(owners_count, capacity, merged_grad.shape[1])
    outgoing_slot = (
        jnp.sum(jnp.where(select, slot_of_row[None, :] + 1, 0), axis=1, dtype=jnp.int32) - 1
    )
    outgoing_slot = outgoing_slot.reshape(owners_count, capacity)
    incoming, incoming_slot = (
        lax.all_to_all(outgoing, CTX, split_axis=0, concat_axis=0, tiled=True),
        lax.all_to_all(outgoing_slot, CTX, split_axis=0, concat_axis=0, tiled=True),
    )
    landing = jnp.arange(slots, dtype=jnp.int32)[:, None] == incoming_slot.reshape(1, slots)
    slotted = jnp.dot(
        landing.astype(jnp.bfloat16),
        incoming.reshape(slots, -1),
        preferred_element_type=jnp.float32,
    )
    slotted = slotted.astype(jnp.bfloat16)
    pre = merger_pre.astype(jnp.float32)
    cdf = 0.5 * (1.0 + lax.erf(pre * 0.5**0.5))
    act = (pre * cdf).astype(jnp.bfloat16)
    slope = cdf + pre * jnp.exp(-0.5 * pre * pre) * (2.0 * math.pi) ** (-0.5)
    linear = lax.dot_general(
        slotted,
        lax.all_gather(fc2_weight, CTX, axis=0, tiled=True),
        (((1,), (1,)), ((), ())),
        preferred_element_type=jnp.float32,
    )
    hidden_grad = (linear * slope).astype(jnp.bfloat16)
    factor = (rows_here * owners_count * replicas) ** (-0.5)
    whole = lax.dot_general(
        act, slotted, (((0,), (0,)), ((), ())), preferred_element_type=jnp.float32
    )
    partial_dp = lax.psum_scatter(whole, "dp", scatter_dimension=1, tiled=True)
    summed = sum_by_axis(partial_dp, CTX, 0)
    weight_grad = summed * factor
    query_grad, key_grad, value_grad = attention_block(
        query, key_states, value_states, out_grad, position
    )
    return (hidden_grad, weight_grad, query_grad, key_grad, value_grad)


def solution(mesh):
    finer = Mesh(mesh.devices.reshape(mesh.shape["dp"], 4, 8), ("dp", "ctx_0", "ctx_1"))
    placed = (
        P(DP_CTX, None),
        P(DP_CTX, None),
        P(DP_CTX, None),
        P(CTX, None),
        P(DP_CTX, None),
        P(DP_CTX, None),
        P(DP_CTX, None),
        P(DP_CTX, None),
        P(None, DP_CTX),
    )
    return jax.shard_map(
        shards,
        mesh=finer,
        in_specs=placed,
        out_specs=(
            P(DP_CTX, None),
            P(CTX, "dp"),
            P(DP_CTX, None),
            P(DP_CTX, None),
            P(DP_CTX, None),
        ),
        check_vma=False,
    )
```

profile of v0, /device:TPU:2, one launch (start us, length us, event | category | flops | bytes accessed | tf_op | source)
XLA Modules:
  0.0 314.4 jit_solution(16009534326722986953)
XLA Ops:
  8.0 0.8 fusion.28
  8.8 0.6 broadcast_in_dim.27
  9.4 11.5 %all-to-all-start = ((s32[32,1,32]{2,1,0:T(1,128)}), s32[32,1,32]{2,1,0:T(1,128)S(1)}, u32[]{:S(2)}, u32[]{:S(2)}) async-start(s32[32,1,32]{2,1,0:T(1,128)} %broadcast_in_dim.27), calls=%async_computation | async-start | bytes 32768 | tf_op jit(solution)/shard_map/all_to_all | solution.py:19
  20.9 0.7 fusion.25
  21.7 0.2 reduce_window_sum.11
  21.9 8.8 %all-to-all-done = s32[32,1,32]{2,1,0:T(1,128)S(1)} async-done(((s32[32,1,32]{2,1,0:T(1,128)}), s32[32,1,32]{2,1,0:T(1,128)S(1)}, u32[]{:S(2)}, u32[]{:S(2)}) %all-to-all-start) | async-done | bytes 4128 | tf_op jit(solution)/shard_map/all_to_all | solution.py:19
  30.9 0.8 select_reduce_fusion.1
  31.8 0.7 add_add_fusion
  32.5 0.7 sub.40
  33.2 3.8 %all-to-all-start.1 = ((s32[32,1,8]{2,1,0:T(1,128)}), s32[32,1,8]{2,1,0:T(1,128)S(1)}, u32[]{:S(2)}, u32[]{:S(2)}) async-start(s32[32,1,8]{2,1,0:T(1,128)} %bitcast.3), calls=%async_computation.1 | async-start | bytes 32768 | tf_op jit(solution)/shard_map/all_to_all | solution.py:144
  37.1 1.3 fusion.9
  38.4 8.4 %all-to-all-done.1 = s32[32,1,8]{2,1,0:T(1,128)S(1)} async-done(((s32[32,1,8]{2,1,0:T(1,128)}), s32[32,1,8]{2,1,0:T(1,128)S(1)}, u32[]{:S(2)}, u32[]{:S(2)}) %all-to-all-start.1) | async-done | bytes 1056 | tf_op jit(solution)/shard_map/all_to_all | solution.py:144
  46.8 3.9 %all-to-all-start.2 = ((bf16[32,8,1792]{2,1,0:T(8,128)(2,1)}), bf16[32,8,1792]{2,1,0:T(8,128)(2,1)S(1)}, u32[]{:S(2)}, u32[]{:S(2)}) async-start(bf16[32,8,1792]{2,1,0:T(8,128)(2,1)} %fusion.9), calls=%async_computation.2 | async-start | bytes 1835008 | tf_op jit(solution)/shard_map/all_to_all | solution.py:143
  50.8 0.5 broadcast.117
  51.3 0.7 reduce.3
  52.1 22.1 %all-to-all-done.2 = bf16[32,8,1792]{2,1,0:T(8,128)(2,1)S(1)} async-done(((bf16[32,8,1792]{2,1,0:T(8,128)(2,1)}), bf16[32,8,1792]{2,1,0:T(8,128)(2,1)S(1)}, u32[]{:S(2)}, u32[]{:S(2)}) %all-to-all-start.2) | async-done | bytes 917536 | tf_op jit(solution)/shard_map/all_to_all | solution.py:143
  74.2 0.4 convolution_convert_fusion.1
  74.6 10.2 %fusion.13 = f32[2560,1792]{0,1:T(8,128)} fusion(bf16[256,1792]{1,0:T(8,128)(2,1)S(1)} %convolution_convert_fusion.1, bf16[256,2560]{1,0:T(8,128)(2,1)} %param.11), kind=kOutput, calls=%fused_computation.28 | convolution fusion | flops 2352742400 | bytes 20578304 | tf_op jit(solution)/shard_map/dot_general | solution.py:165
  85.0 96.0 %reduce-scatter.6.cloned.1.call-done = f32[2560,224]{0,1:T(8,128)} async-done(((f32[2560,1792]{0,1:T(8,128)}), f32[2560,224]{0,1:T(8,128)}) %reduce-scatter.6.cloned.1.call-update) | async-done | bytes 2293776 | tf_op jit(solution)/shard_map/reduce_scatter | solution.py:168
  181.0 0.5 all-gather.2.cloned.1.call-update
  181.6 2.5 reshape.195
  184.2 2.5 reshape.194
  186.7 1.3 copy.70
  188.0 0.1 convert.38
  188.2 1.3 copy.73
  189.5 0.1 convert.39
  189.7 0.2 broadcast_multiply_fusion.1
  189.9 1.2 subtract_convert_fusion.3
  191.1 1.3 concatenate.42
  192.4 0.7 copy.72
  193.2 1.2 concatenate.41
  194.3 1.6 copy.71
  196.0 2.4 concatenate.45
  198.4 2.3 copy.75
  200.7 1.1 concatenate.44
  201.8 2.3 copy.74
  204.1 4.6 %fusion.41 = (f32[4,16,64]{2,1,0:T(8,128)S(1)}, f32[4,16,64,64]{2,3,1,0:T(8,128)}) fusion(bf16[4,64,16,40]{3,1,2,0:T(8,128)(2,1)S(1)} %copy.72, bf16[4,64,16,40]{3,1,2,0:T(8,128)(2,1)S(1)} %copy.71, bf16[4,64,16,40]{3,1,2,0:T(8,128)(2,1)} %copy.75, bf16[4,64,16,40]{3,1,2,0:T(8,128)(2,1)} %copy.74), kind=kOutput, calls=%fused_computation.83 | convolution fusion | flops 45350976 | bytes 2375680 | tf_op jit(solution)/shard_map/sub | solution.py:89
  208.7 3.4 %fusion.10 = f32[4,64,16]{1,2,0:T(8,128)S(1)} fusion(bf16[4,64,16,80]{3,2,1,0:T(8,128)(2,1)} %reshape.195, bf16[4,64,16,80]{3,2,1,0:T(8,128)(2,1)} %reshape.194, f32[4,16,64,64]{2,3,1,0:T(8,128)} %get-tuple-element.53, f32[4,16,64]{2,1,0:T(8,128)S(1)} %get-tuple-element.52), kind=kOutput, calls=%fused_computation.19 | convolution fusion | flops 43446272 | bytes 2392064 | tf_op jit(solution)/shard_map/whqk,wkhd->wqhd/dot_general | solution.py:91
  212.3 0.7 multiply_convert_fusion
  213.0 0.5 copy-done.5
  213.5 0.3 copy-done.6
  213.8 0.7 multiply_bitcast_fusion
  214.6 0.2 copy-done.2
  214.8 1.2 copy.86
  216.0 2.1 fusion.39
  218.1 3.3 %copy.102 = f32[256,16,40]{0,2,1:T(8,128)} copy(f32[256,16,40]{2,1,0:T(8,128)} %get-tuple-element.29) | data formatting | bytes 1310720
  221.4 1.8 copy.101
  223.3 2.8 multiply_bitcast_fusion.1
  226.1 1.2 copy.83
  227.3 2.1 fusion.40
  229.4 3.5 %copy.99 = f32[256,16,40]{0,2,1:T(8,128)} copy(f32[256,16,40]{2,1,0:T(8,128)} %get-tuple-element.32) | data formatting | bytes 1310720
  233.0 1.8 copy.100
  234.8 2.0 subtract_convert_fusion
  236.8 0.1 pad_maximum_fusion.2
  237.0 1.1 copy.92
  238.0 1.1 copy.93
  239.1 2.1 copy.97
  241.3 2.7 fusion.12
  243.9 0.7 copy.90
  244.6 2.0 reshape.198
  246.7 50.9 %all-gather.2.cloned.1.call-done = bf16[2560,1792]{1,0:T(8,128)(2,1)} async-done(((bf16[80,1792]{1,0:T(8,128)(2,1)}), bf16[2560,1792]{1,0:T(8,128)(2,1)}) %all-gather.2.cloned.1.call-update) | async-done | bytes 9175056 | tf_op jit(solution)/shard_map/all_gather | solution.py:159
  297.5 8.0 %fusion.1 = bf16[256,2560]{1,0:T(8,128)(2,1)} fusion(bf16[256,1792]{1,0:T(8,128)(2,1)S(1)} %convolution_convert_fusion.1, bf16[2560,1792]{1,0:T(8,128)(2,1)} %all-gather.2.cloned.1.call-done, bf16[256,2560]{1,0:T(8,128)(2,1)} %param.11), kind=kOutput, calls=%fused_computation.7 | convolution fusion | flops 2356019200 | bytes 12713984 | tf_op jit(solution)/shard_map/dot_general | solution.py:157
  305.5 1.0 copy.98
  306.5 0.7 copy.91
  (54 shorter events, 1.0 us)
Async XLA Ops:
  8.0 29.1 %copy-start = (bf16[128,1792]{1,0:T(8,128)(2,1)S(1)}, bf16[128,1792]{1,0:T(8,128)(2,1)}, u32[]{:S(2)}) copy-start(bf16[128,1792]{1,0:T(8,128)(2,1)} %param.9) | copy-start | bytes 1376260
  9.4 21.2 %all-to-all-start = ((s32[32,1,32]{2,1,0:T(1,128)}), s32[32,1,32]{2,1,0:T(1,128)S(1)}, u32[]{:S(2)}, u32[]{:S(2)}) async-start(s32[32,1,32]{2,1,0:T(1,128)} %broadcast_in_dim.27), calls=%async_computation | async-start | bytes 32768 | tf_op jit(solution)/shard_map/all_to_all | solution.py:19
  33.2 13.5 %all-to-all-start.1 = ((s32[32,1,8]{2,1,0:T(1,128)}), s32[32,1,8]{2,1,0:T(1,128)S(1)}, u32[]{:S(2)}, u32[]{:S(2)}) async-start(s32[32,1,8]{2,1,0:T(1,128)} %bitcast.3), calls=%async_computation.1 | async-start | bytes 32768 | tf_op jit(solution)/shard_map/all_to_all | solution.py:144
  46.8 27.4 %all-to-all-start.2 = ((bf16[32,8,1792]{2,1,0:T(8,128)(2,1)}), bf16[32,8,1792]{2,1,0:T(8,128)(2,1)S(1)}, u32[]{:S(2)}, u32[]{:S(2)}) async-start(bf16[32,8,1792]{2,1,0:T(8,128)(2,1)} %fusion.9), calls=%async_computation.2 | async-start | bytes 1835008 | tf_op jit(solution)/shard_map/all_to_all | solution.py:143
  50.7 130.2 %reduce-scatter.6.cloned.1.call-start = ((), (), s32[]{:S(2)}) async-start(), calls=%async_computation.7 | async-start | bytes 20643840 | tf_op jit(solution)/shard_map/reduce_scatter | solution.py:168
  84.9 96.7 %copy-start.9 = (bf16[256,1280]{1,0:T(8,128)(2,1)S(1)}, bf16[256,1280]{1,0:T(8,128)(2,1)}, u32[]{:S(2)}) copy-start(bf16[256,1280]{1,0:T(8,128)(2,1)} %param.15) | copy-start | bytes 1966084
  84.9 154.2 %reduce-scatter.8.cloned.1.call-start = ((), (), s32[]{:S(2)}) async-start(), calls=%async_computation.8 | async-start | bytes 2867200 | tf_op jit(solution)/shard_map/reduce_scatter | solution.py:45
  180.9 3.2 %copy-start.10 = (bf16[256,1280]{1,0:T(8,128)(2,1)S(1)}, bf16[256,1280]{1,0:T(8,128)(2,1)}, u32[]{:S(2)}) copy-start(bf16[256,1280]{1,0:T(8,128)(2,1)} %param.16) | copy-start | bytes 1966084
  181.0 116.6 %all-gather.2.cloned.1.call-start = ((), (), s32[]{:S(2)}) async-start(), calls=%async_computation.6 | async-start | bytes 9461760 | tf_op jit(solution)/shard_map/all_gather | solution.py:159
  181.6 123.9 %reduce-scatter.10.cloned.1.call-start = ((), (), s32[]{:S(2)}) async-start(), calls=%async_computation.9 | async-start | bytes 737280
  188.1 1.5 copy-start.11
  193.2 10.9 %copy-start.3 = (bf16[4,64,16,40]{3,1,2,0:T(8,128)(2,1)}, bf16[4,64,16,40]{3,1,2,0:T(8,128)(2,1)S(1)}, u32[]{:S(2)}) copy-start(bf16[4,64,16,40]{3,1,2,0:T(8,128)(2,1)S(1)} %copy.72) | copy-start | bytes 983044
  195.9 8.2 %copy-start.4 = (bf16[4,64,16,40]{3,1,2,0:T(8,128)(2,1)}, bf16[4,64,16,40]{3,1,2,0:T(8,128)(2,1)S(1)}, u32[]{:S(2)}) copy-start(bf16[4,64,16,40]{3,1,2,0:T(8,128)(2,1)S(1)} %copy.71) | copy-start | bytes 983044
  208.7 3.4 %copy-start.7 = (bf16[4,64,16,80]{3,2,1,0:T(8,128)(2,1)S(1)}, bf16[4,64,16,80]{3,2,1,0:T(8,128)(2,1)}, u32[]{:S(2)}) copy-start(bf16[4,64,16,80]{3,2,1,0:T(8,128)(2,1)} %reshape.194) | copy-start | bytes 1966084
  208.7 3.4 %copy-start.8 = (bf16[4,64,16,80]{3,2,1,0:T(8,128)(2,1)S(1)}, bf16[4,64,16,80]{3,2,1,0:T(8,128)(2,1)}, u32[]{:S(2)}) copy-start(bf16[4,64,16,80]{3,2,1,0:T(8,128)(2,1)} %reshape.195) | copy-start | bytes 1966084
  208.7 3.6 %copy-start.12 = (f32[4,16,64,64]{2,3,1,0:T(8,128)S(1)}, f32[4,16,64,64]{2,3,1,0:T(8,128)}, u32[]{:S(2)}) copy-start(f32[4,16,64,64]{2,3,1,0:T(8,128)} %get-tuple-element.53) | copy-start | bytes 3145732
  212.3 1.2 copy-start.5
  212.3 1.6 copy-start.6
  213.8 1.0 copy-start.2
  297.5 9.7 %copy-start.1 = (bf16[128,1792]{1,0:T(8,128)(2,1)S(1)}, bf16[128,1792]{1,0:T(8,128)(2,1)}, u32[]{:S(2)}) copy-start(bf16[128,1792]{1,0:T(8,128)(2,1)} %param.9) | copy-start | bytes 1376260
Sparse Core Ops, SparseCore 0:
  85.0 95.8 reduce-scatter.5
  183.5 39.5 reduce-scatter.7
  241.4 56.9 reduce-scatter.9
Sparse Core Ops, SparseCore 1:
  184.0 113.4 all-gather.1
where the time goes:
time: 315 us; the launch traced here: 314 us
  waiting for transfers between devices  187 us (59%)
  local copies, waits for them, and re-layouts  49.8 us (16%)
  matrix products  34.9 us (11%)
  starting transfers between devices  19.4 us (6%)
  between operations  15.5 us (5%)
  other arithmetic  8.01 us (3%)
    reduce_scatter x1, waiting for transfers between devices, shards(): partial_dp = lax.psum_scatter(whole, 'dp', scatter_dimension=1, tiled=True)  96 us
    all_gather x1, waiting for transfers between devices, shards(): lax.all_gather(fc2_weight, CTX, axis=0, tiled=True)  50.9 us
    all_to_all x1, waiting for transfers between devices, shards(): lax.all_to_all(outgoing, CTX, split_axis=0, concat_axis=0, tiled=True)  22.1 us
    unnamed x37, local copies, waits for them, and re-layouts  20.4 us
    concatenate x8, local copies, waits for them, and re-layouts, rotate(): jnp.concatenate([first * cosine - second * sine, second * cosine + first...  12.9 us
    all_to_all x1, starting transfers between devices, sent_to_all(): return lax.all_to_all(copies, axis, split_axis=0, concat_axis=0, tiled=True)  11.5 us
    dot_general x1, matrix products, shards(): lax.dot_general(act, slotted, (((0,), (0,)), ((), ())), preferred_element...  10.2 us
    all_to_all x1, waiting for transfers between devices, sent_to_all(): return lax.all_to_all(copies, axis, split_axis=0, concat_axis=0, tiled=True)  8.77 us
  transfers between devices with their start and end apart: 7, of which 5 were waited for; matrix products, arithmetic and copies ran while one was open for 24% of the time, Pallas kernels for 0%

commit v1 on v0

v1 whole, which is shorter than its diff:
```python
import functools
import math

import jax
import jax.numpy as jnp
from jax import lax
from jax.experimental import pallas as pl
from jax.experimental.pallas import tpu as pltpu
from jax.sharding import Mesh
from jax.sharding import PartitionSpec as P

HEAD = 80
WIN = 64
CTX = ("y", "z")
DP = ("x", "k")
ALL = ("x", "k", "y", "z")
F32 = jnp.float32
BF16 = jnp.bfloat16
MIB = 1024 * 1024


def iota(shape, dim):
    return lax.broadcasted_iota(jnp.int32, shape, dim)


def mm(a, b):
    return lax.dot_general(a, b, (((1,), (0,)), ((), ())), preferred_element_type=F32)


def mm_nt(a, b):
    return lax.dot_general(a, b, (((1,), (1,)), ((), ())), preferred_element_type=F32)


def mm_tn(a, b):
    return lax.dot_general(a, b, (((0,), (0,)), ((), ())), preferred_element_type=F32)


def shifted(n, s):
    return [(i, (i + s) % n) for i in range(n)]


def after(v, *others):
    return lax.optimization_barrier((v, *others))[0]


def params(mib=40):
    return pltpu.CompilerParams(vmem_limit_bytes=mib * MIB)


def cost(flops, nbytes, trans=0):
    return pl.CostEstimate(flops=flops, bytes_accessed=nbytes, transcendentals=trans)


def pack_kernel(cap, own_ref, grad_ref, out_ref):
    rows, width = grad_ref.shape
    places = out_ref.shape[0]
    owner = own_ref[...]
    onehot = (owner == iota((rows, 128), 1)).astype(F32)
    earlier = (iota((rows, rows), 0) > iota((rows, rows), 1)).astype(BF16)
    before = mm(earlier, onehot.astype(BF16))
    rank = jnp.sum(before * onehot, axis=1, keepdims=True).astype(jnp.int32)
    target = owner * cap + rank
    select = (target == iota((rows, places), 1)).astype(F32).T.astype(BF16)
    out_ref[:, :width] = mm(select, grad_ref[...]).astype(BF16)
    out_ref[:, width:] = mm(select, jnp.ones((rows, 128), BF16)).astype(BF16)


def packed(owner, grad, places, cap):
    rows, width = grad.shape
    return pl.pallas_call(
        functools.partial(pack_kernel, cap),
        out_shape=jax.ShapeDtypeStruct((places, width + 128), BF16),
        compiler_params=params(),
        cost_estimate=cost(2 * places * rows * width, 2 * (places + rows) * width),
        name="pack",
    )(owner, grad)


def land_kernel(inc_ref, out_ref, blocks_ref):
    slots, width = out_ref.shape
    parts, part, _ = blocks_ref.shape
    flags = inc_ref[:, width:].astype(F32).T.astype(BF16)
    earlier = (iota((slots, slots), 0) < iota((slots, slots), 1)).astype(BF16)
    slot = mm(flags[:16], earlier)[:1].astype(jnp.int32)
    here = flags[:1].astype(F32) > 0.5
    slot = jnp.where(here, slot, -1)
    landing = (iota((slots, slots), 0) == slot).astype(BF16)
    rows = mm(landing, inc_ref[:, :width])
    out_ref[...] = rows.astype(BF16)
    blocks_ref[...] = rows.T.astype(BF16).reshape(blocks_ref.shape)


def landed(incoming, parts):
    slots, wide = incoming.shape
    width = wide - 128
    return pl.pallas_call(
        land_kernel,
        out_shape=(
            jax.ShapeDtypeStruct((slots, width), BF16),
            jax.ShapeDtypeStruct((parts, width // parts, slots), BF16),
        ),
        compiler_params=params(),
        cost_estimate=cost(2 * slots * slots * width, 6 * slots * width),
        name="land",
    )(incoming)


def act_kernel(pre_ref, out_ref):
    x = pre_ref[...].astype(F32)
    act = x * (0.5 * (1.0 + lax.erf(x * 0.5**0.5)))
    out_ref[...] = act.T.astype(BF16)


def activated(pre):
    slots, hid = pre.shape
    block = hid // 4
    return pl.pallas_call(
        act_kernel,
        grid=(4,),
        in_specs=[pl.BlockSpec((slots, block), lambda i: (0, i))],
        out_specs=pl.BlockSpec((block, slots), lambda i: (i, 0)),
        out_shape=jax.ShapeDtypeStruct((hid, slots), BF16),
        compiler_params=params(),
        cost_estimate=cost(40 * slots * hid, 4 * slots * hid),
        name="act",
    )(pre)


def hidden_kernel(at_ref, slot_ref, pre_ref, *refs):
    *lines, out_ref, held, sems = refs
    step = pl.program_id(0)
    owners = at_ref.shape[0] // 4

    @pl.when(step == 0)
    def _():
        first = 0
        copies = []
        for i, ref in enumerate(lines):
            count = ref.shape[0]
            into = held.at[pl.ds(first, count)]
            copies.append(pltpu.make_async_copy(ref, into, sems.at[i]))
            first += count
        for copy in copies:
            copy.start()
        for copy in copies:
            copy.wait()

    rows = [held[at_ref[step * owners + i]] for i in range(owners)]
    linear = mm_nt(slot_ref[...], jnp.concatenate(rows, axis=0))
    x = pre_ref[...].astype(F32)
    slope = 0.5 * (1.0 + lax.erf(x * 0.5**0.5))
    slope = slope + x * jnp.exp(-0.5 * x * x) * (2.0 * math.pi) ** -0.5
    out_ref[...] = (linear * slope).astype(BF16)


def hidden_of(at, slotted, pre, lines):
    slots, width = slotted.shape
    hid = pre.shape[1]
    block = hid // 4
    return pl.pallas_call(
        hidden_kernel,
        grid_spec=pltpu.PrefetchScalarGridSpec(
            num_scalar_prefetch=1,
            grid=(4,),
            in_specs=[
                pl.BlockSpec((slots, width), lambda i, s: (0, 0)),
                pl.BlockSpec((slots, block), lambda i, s: (0, i)),
                *[pl.BlockSpec(memory_space=pl.ANY)] * len(lines),
            ],
            out_specs=pl.BlockSpec((slots, block), lambda i, s: (0, i)),
            scratch_shapes=[
                pltpu.VMEM((at.shape[0], *lines[0].shape[1:]), BF16),
                pltpu.SemaphoreType.DMA((len(lines),)),
            ],
        ),
        out_shape=jax.ShapeDtypeStruct((slots, hid), BF16),
        compiler_params=params(58),
        cost_estimate=cost(2 * slots * width * hid, 2 * (hid * width + 2 * slots * hid)),
        name="hidden",
    )(at, slotted, pre, *lines)


def weight_kernel(scale, idx_ref, cols_ref, own, mine, other, mine_half, other_half, *refs):
    outs, cols = refs[:5], refs[5]
    step = pl.program_id(0)
    slots = own.shape[2]

    @pl.when(step == 0)
    def _():
        for j in range(8):
            cols[j * slots : (j + 1) * slots] = cols_ref[idx_ref[j]].astype(F32).T.astype(BF16)

    ours = idx_ref[12 + step] == 1
    across = [jnp.where(ours, mine_half[i], other_half[1 - i]) for i in (0, 1)]
    rows = [own[0], own[1], mine[0], mine[1], other[0], other[1], *across]
    total = mm(jnp.concatenate(rows, axis=1), cols[...]) * scale

    @pl.when(step == 0)
    def _():
        cut = total.shape[0] // 2
        outs[0][...] = total[:cut]
        outs[1][...] = total[cut:]

    for q in range(3):

        @pl.when(step == q + 1)
        def _(q=q):
            cut = total.shape[0] // 2
            outs[2 + q][0] = total[:cut]
            outs[2 + q][1] = total[cut:]


def weight_rows(idx, cols, own, mine, other, mine_half, other_half, scale):
    _, hid, slots = own.shape
    part = cols.shape[1]
    block = hid // 4

    def whole(shape):
        return pl.BlockSpec(shape, lambda i, s: (0,) * len(shape))

    full = pl.BlockSpec((2, block, slots), lambda i, s: (0, s[8 + i], 0))
    half = pl.BlockSpec((2, block, slots), lambda i, s: (0, s[8 + i] % 2, 0))
    shapes = [(block // 2, part)] * 2 + [(2, block // 2, part)] * 3
    return pl.pallas_call(
        functools.partial(weight_kernel, scale),
        grid_spec=pltpu.PrefetchScalarGridSpec(
            num_scalar_prefetch=1,
            grid=(4,),
            in_specs=[whole(cols.shape), full, full, full, half, half],
            out_specs=[whole(shape) for shape in shapes],
            scratch_shapes=[pltpu.VMEM((8 * slots, part), BF16)],
        ),
        out_shape=[jax.ShapeDtypeStruct(shape, F32) for shape in shapes],
        compiler_params=params(),
        cost_estimate=cost(2 * hid * slots * 8 * part, 2 * hid * slots * 8 + 4 * hid * part),
        name="weight",
    )(idx, cols, own, mine, other, mine_half, other_half)


def add_kernel(rows_ref, add_ref, out_ref):
    out_ref[0] = rows_ref[0] + add_ref[...]


def added(rows, addend, at):
    block = pl.BlockSpec((1, *addend.shape), lambda i: (at, 0, 0))
    return pl.pallas_call(
        add_kernel,
        grid=(1,),
        in_specs=[block, pl.BlockSpec(addend.shape, lambda i: (0, 0))],
        out_specs=block,
        out_shape=jax.ShapeDtypeStruct(rows.shape, rows.dtype),
        input_output_aliases={0: 0},
        compiler_params=params(),
        cost_estimate=cost(addend.size, 12 * addend.size),
        name="add",
    )(rows, addend)


def attention_kernel(q_ref, k_ref, v_ref, g_ref, cos_ref, sin_ref, *refs):
    qg_ref, kg_ref, vg_ref, *scratch = refs[-7:]
    qr_ref, kr_ref = scratch[:2]
    dq_ref, dk_ref = scratch[2:]
    win, width = q_ref.shape
    half_width = width // 2
    factor = HEAD**-0.5
    lane = iota((win, half_width), 1)
    first = lane % HEAD < HEAD // 2
    count = HEAD // 2
    spread = (iota((count, half_width), 1) % count == iota((count, half_width), 0)).astype(F32)

    def spread_out(table):
        dims = (((1,), (0,)), ((), ()))
        return lax.dot_general(
            table, spread, dims, precision=lax.Precision.HIGHEST, preferred_element_type=F32
        )

    cos = spread_out(cos_ref[...])
    sin = spread_out(sin_ref[...])
    sin = jnp.where(first, -sin, sin)

    def turned(x):
        left = pltpu.roll(x, half_width - HEAD // 2, 1)
        right = pltpu.roll(x, HEAD // 2, 1)
        return jnp.where(first, left, right) * sin

    for s in range(2):
        at = pl.ds(s * half_width, half_width)
        for src, dst in ((q_ref, qr_ref), (k_ref, kr_ref)):
            x = src[:, at].astype(F32)
            dst[:, at] = (x * cos + turned(x)).astype(BF16)
    wide = 256
    span = iota((win, wide), 1)
    for pair in range(width // (2 * HEAD)):
        start = pair * 2 * HEAD
        base = start // 128 * 128
        at = pl.ds(base, wide)
        lo = start - base
        one = (span >= lo) & (span < lo + HEAD)
        two = (span >= lo + HEAD) & (span < lo + 2 * HEAD)

        def stacked(x):
            x = x.astype(F32)
            zero = jnp.zeros_like(x)
            return jnp.concatenate([jnp.where(one, x, zero), jnp.where(two, x, zero)], 0).astype(BF16)

        q2 = stacked(qr_ref[:, at])
        g2 = stacked(g_ref[:, at])
        kk = kr_ref[:, at]
        scores = mm_nt(kk, q2)
        top = jnp.max(scores, axis=0, keepdims=True)
        e = jnp.exp((scores - top) * factor)
        probs = e * (1.0 / jnp.sum(e, axis=0, keepdims=True))
        probs_b = probs.astype(BF16)
        prob_grad = mm_nt(v_ref[:, at], g2)
        delta = jnp.sum(probs_b.astype(F32) * prob_grad, axis=0, keepdims=True)
        score_f = probs * (prob_grad - delta)
        score_grad = score_f.astype(BF16)
        vg = mm(probs_b, g2)
        kg = mm(score_grad, q2)
        qg = mm(score_f.T.astype(BF16), kk)
        qg = jnp.where(one, qg[:win], qg[win:])
        both = one | two
        for ref, val in ((vg_ref, vg), (dk_ref, kg), (dq_ref, qg)):
            if lo:
                old = ref[:, pl.ds(base, 128)]
                new = jnp.where(both[:, :128], val[:, :128].astype(old.dtype), old)
                ref[:, pl.ds(base, 128)] = new
                ref[:, pl.ds(base + 128, 128)] = val[:, 128:].astype(old.dtype)
            else:
                ref[:, at] = val.astype(ref.dtype)
    for s in range(2):
        at = pl.ds(s * half_width, half_width)
        for src, dst in ((dq_ref, qg_ref), (dk_ref, kg_ref)):
            x = src[:, at] * factor
            dst[:, at] = (x * cos - turned(x)).astype(BF16)


def attention(first, windows, query, key_states, value_states, out_grad, cos, sin, *earlier):
    count, width = query.shape
    block = pl.BlockSpec((WIN, width), lambda w: (w + first, 0))
    table = pl.BlockSpec((WIN, HEAD // 2), lambda w: (w + first, 0))
    out = jax.ShapeDtypeStruct((count, width), BF16)
    return pl.pallas_call(
        attention_kernel,
        grid=(windows,),
        in_specs=[block] * 4 + [table] * 2 + [pl.BlockSpec(memory_space=pl.ANY)] * len(earlier),
        out_specs=[block] * 3,
        out_shape=[out] * 3,
        scratch_shapes=[pltpu.VMEM((WIN, width), BF16)] * 2 + [pltpu.VMEM((WIN, width), F32)] * 2,
        input_output_aliases={6 + i: i for i in range(len(earlier))},
        compiler_params=params(58),
        cost_estimate=cost(160 * windows * WIN * WIN * width, 18 * windows * WIN * width),
        name="attention",
    )(query, key_states, value_states, out_grad, cos, sin, *earlier)


def rope_tables(position):
    quarter = HEAD // 4
    freq = 1.0 / 10000.0 ** (jnp.arange(quarter, dtype=F32) * (4.0 / HEAD))
    rows = position[0].astype(F32)[:, None] * freq[None, :]
    cols = position[1].astype(F32)[:, None] * freq[None, :]
    angles = jnp.concatenate([rows, cols], axis=1)
    return jnp.cos(angles), jnp.sin(angles)


def shards(merged_grad, merged_owner, pre, fc2, query, key_states, value_states, out_grad, position):
    owners, replicas = lax.axis_size(CTX), lax.axis_size(DP)
    xs, ys, zs = (lax.axis_size(axis) for axis in ("x", "y", "z"))
    x, k, y, z = (lax.axis_index(axis) for axis in ALL)
    slots, hid = pre.shape
    rows_here = merged_grad.shape[0]
    cap = slots // owners

    def hop(v, axis, by):
        return lax.ppermute(v, axis, shifted(lax.axis_size(axis), by))

    def apart(v, axis):
        n = lax.axis_size(axis)
        steps = [(core, i, (i + 1 - 2 * core) % n) for core in (0, 1) for i in range(n)]
        if axis == "x":
            return lax.ppermute(v, DP, [(2 * i + core, 2 * j + core) for core, i, j in steps])
        return lax.ppermute(v, ("k", axis), [(n * core + i, n * core + j) for core, i, j in steps])

    def numbers(*values):
        return jnp.stack(values).astype(jnp.int32)

    outgoing = packed(merged_owner, merged_grad, slots, cap)
    incoming = lax.all_to_all(
        outgoing.reshape(owners, cap, -1), CTX, split_axis=0, concat_axis=0, tiled=True
    )

    act = activated(after(pre, outgoing))
    own = jnp.stack([act, hop(act, "k", 1)])
    mine = apart(own, "x")

    line = after(fc2, act)
    beside = [hop(line, "y", by) for by in range(1, ys)]

    tables = rope_tables(position)
    grads = attention(0, 2, after(query, act), key_states, value_states, out_grad, *tables)

    grads = attention(
        2, 2, after(query, own), key_states, value_states, out_grad, *tables, *grads
    )
    mine = after(mine, *grads, *beside)
    mine_half = lax.dynamic_slice_in_dim(mine, k * (hid // 2), hid // 2, axis=1)
    mine_half = apart(mine_half, "x")

    slotted, blocks = landed(after(incoming, *grads).reshape(slots, -1), replicas)
    cols = lax.all_to_all(blocks, DP, split_axis=0, concat_axis=0, tiled=True)
    mine_half = after(mine_half, cols)
    other, other_half = hop(mine, "k", 1), hop(mine_half, "k", 1)

    before, behind = (x - 1 + 2 * k) % xs, (x + 1 - 2 * k) % xs
    places = []
    for there, core in ((x, k), (before, k), (behind, 1 - k), ((x + 2) % xs, k)):
        places += [2 * there + core, 2 * there + 1 - core]
    quarters = [(y + dy) % ys for dy in (2, 1, 3, 0)]
    ours = [(q < 2) == (k == 0) for q in quarters]
    factor = (rows_here * owners * replicas) ** (-0.5)
    idx = numbers(*places, *quarters, *ours)
    top, bottom, above, below, here = weight_rows(
        idx, cols, own, mine, other, mine_half, other_half, factor
    )
    from_below, from_above = hop(top, "y", 1), hop(bottom, "y", -1)
    above = hop(added(above, from_below, 0), "y", 1)
    below = hop(added(below, from_above, 1), "y", -1)

    line = jnp.stack([line, *beside])
    ones = [apart(after(line, slotted), "z")]
    ones.append(apart(ones[0], "z"))
    ones.append(apart(after(ones[1], from_below, from_above), "z"))
    last = lax.dynamic_slice_in_dim(ones[2], k * (ys // 2), ys // 2, axis=0)
    ones.append(apart(last, "z"))
    lines = [line, *ones, *(hop(part, "k", 1) for part in ones)]

    turn = (y - jnp.arange(ys))[:, None] % ys
    away = (jnp.arange(zs)[None, :] - z) % zs
    by_core = jnp.where(away == 4, turn >= 2, away < 4).astype(jnp.int32)
    step = jnp.where(away < 4, away, zs - away)
    at = jnp.where(away == 4, 12 + turn % 2, 4 * step - 4 + turn)
    at = jnp.where(by_core == k, 4, 18) + at
    at = jnp.where(away == 0, turn, at).astype(jnp.int32).reshape(-1)
    hidden_grad = hidden_of(at, slotted, pre, lines)

    total = here + above + below
    pieces = total.reshape(zs, hid // owners, -1)
    pieces = lax.all_to_all(pieces, "z", split_axis=0, concat_axis=0, tiled=True)
    weight_grad = jnp.sum(after(pieces, hidden_grad), axis=0)
    return (hidden_grad, weight_grad, *grads)


def solution(mesh):
    finer = Mesh(mesh.devices.reshape(4, 2, 4, 8), ALL)
    rows = P(ALL, None)
    return jax.shard_map(
        shards,
        mesh=finer,
        in_specs=(rows, rows, rows, P(CTX, None), rows, rows, rows, rows, P(None, ALL)),
        out_specs=(rows, P(CTX, DP), rows, rows, rows),
        check_vma=False,
    )
```

time: 315 us -> 148 us (0.47)
  waiting for transfers between devices: 187 us -> 49.9 us
  Pallas kernels: 0 us -> 41 us
  local copies, waits for them, and re-layouts: 49.8 us -> 10.2 us
  matrix products: 34.9 us -> 0 us
  starting transfers between devices: 19.4 us -> 39.2 us
  between operations: 15.5 us -> 0.87 us
    reduce_scatter x2 -> x0, waiting for transfers between devices: 96 us -> none  [the longest x1 96 us: shards(): partial_dp = lax.psum_scatter(whole, 'dp', scatter_dimension=1, tiled=True)]
    all_gather x1 -> x0, waiting for transfers between devices: 50.9 us -> none  [shards(): lax.all_gather(fc2_weight, CTX, axis=0, tiled=True)]
    pallas_call x0 -> x9, Pallas kernels: none -> 41 us  [the longest x2 14.8 us: attention(): pl.pallas_call(attention_kernel, grid=(windows,), in_specs=[block] * 4 +...]
    ppermute x0 -> x20, waiting for transfers between devices: none -> 30.6 us  [the longest x4 24.4 us: apart(): lax.ppermute(v, ('k', axis), [(n * core + i, n * core + j) for core, i, j...]
    dot_general x9 -> x0, matrix products: 30.3 us -> none  [the longest x1 10.2 us: shards(): lax.dot_general(act, slotted, (((0,), (0,)), ((), ())), preferred_element...]
    all_to_all x3, waiting for transfers between devices: 39.3 us -> 19.2 us  [the longest x1 9.15 us: shards(): cols = lax.all_to_all(blocks, DP, split_axis=0, concat_axis=0, tiled=True)]
    ppermute x0 -> x20, starting transfers between devices: none -> 18.1 us  [the longest x14 12.9 us: hop(): return lax.ppermute(v, axis, shifted(lax.axis_size(axis), by))]
    unnamed x37 -> x25, local copies, waits for them, and re-layouts: 20.4 us -> 4.59 us
  transfers between devices with their start and end apart: 7 -> 23, of which waited for: 5 -> 11; matrix products, arithmetic and copies ran while one was open for 24% -> 7% of each run, Pallas kernels for 0% -> 27%
where the time goes in v1:
time: 148 us; the launch traced here: 146 us
  waiting for transfers between devices  49.9 us (34%)
  Pallas kernels  41 us (28%)
  starting transfers between devices  39.2 us (26%)
  local copies, waits for them, and re-layouts  10.2 us (7%)
  other arithmetic  5.06 us (3%)
    ppermute x4, waiting for transfers between devices, apart(): lax.ppermute(v, ('k', axis), [(n * core + i, n * core + j) for core, i, j...  24.4 us
    pallas_call x2, Pallas kernels, attention(): pl.pallas_call(attention_kernel, grid=(windows,), in_specs=[block] * 4 +...  14.8 us
    ppermute x14, starting transfers between devices, hop(): return lax.ppermute(v, axis, shifted(lax.axis_size(axis), by))  12.9 us
    pallas_call x1, Pallas kernels, hidden_of(): pl.pallas_call(hidden_kernel, grid_spec=pltpu.PrefetchScalarGridSpec(num_...  10.3 us
    all_to_all x1, waiting for transfers between devices, shards(): cols = lax.all_to_all(blocks, DP, split_axis=0, concat_axis=0, tiled=True)  9.15 us
    all_to_all x1, starting transfers between devices, shards(): lax.all_to_all(outgoing.reshape(owners, cap, -1), CTX, split_axis=0, conc...  9.09 us
    pallas_call x1, Pallas kernels, weight_rows(): pl.pallas_call(functools.partial(weight_kernel, scale), grid_spec=pltpu.P...  8.52 us
    ppermute x14, waiting for transfers between devices, hop(): return lax.ppermute(v, axis, shifted(lax.axis_size(axis), by))  6.23 us
  transfers between devices with their start and end apart: 23, of which 11 were waited for; matrix products, arithmetic and copies ran while one was open for 7% of the time, Pallas kernels for 27%

profile of v1, /device:TPU:2, one launch (start us, length us, event | category | flops | bytes accessed | tf_op | source)
XLA Modules:
  0.0 146.2 jit_solution(5953546443967311972)
XLA Ops:
  0.6 0.0 copy-start
  0.6 0.9 copy.20.own_ref
  1.5 1.0 copy-done.6
  2.5 0.8 pack.1
  3.4 1.1 act.1
  4.5 0.1 collective-permute-start
  4.6 3.0 %collective-permute-done = bf16[2560,256]{1,0:T(8,128)(2,1)S(1)} collective-permute-done((bf16[2560,256]{1,0:T(8,128)(2,1)S(1)}, bf16[2560,256]{1,0:T(8,128)(2,1)S(1)}, u32[]{:S(2)}, u32[]{:S(2)}) %collective-permute-start) | collective-permute-done | bytes 1310752 | tf_op jit(solution)/shard_map/ppermute | solution.py:375
  7.6 0.2 pad_maximum_fusion.own
  7.9 1.6 %collective-permute-start.6 = (bf16[2,2560,256]{2,1,0:T(8,128)(2,1)S(1)}, bf16[2,2560,256]{2,1,0:T(8,128)(2,1)}, u32[]{:S(2)}, u32[]{:S(2)}) collective-permute-start(bf16[2,2560,256]{2,1,0:T(8,128)(2,1)S(1)} %pad_maximum_fusion.own), channel_id=1, source_target_pairs={{0,64},{64,128},{128,192},{192,0},{32,224},{96,32},{160,96},{224,1... | collective-permute-start | bytes 7864328 | tf_op jit(solution)/shard_map/ppermute | solution.py:381
  9.4 1.6 %collective-permute-start.1 = (bf16[80,1792]{1,0:T(8,128)(2,1)S(1)}, bf16[80,1792]{1,0:T(8,128)(2,1)S(1)}, u32[]{:S(2)}, u32[]{:S(2)}) collective-permute-start(bf16[80,1792]{1,0:T(8,128)(2,1)S(1)} %copy-done.9), channel_id=1, source_target_pairs={{0,8},{8,16},{16,24},{24,0},{1,9},{9,17},{17,25},{25,1},{2,10},{10... | collective-permute-start | bytes 860168 | tf_op jit(solution)/shard_map/ppermute | solution.py:375
  11.0 2.9 %collective-permute-start.2 = (bf16[80,1792]{1,0:T(8,128)(2,1)S(1)}, bf16[80,1792]{1,0:T(8,128)(2,1)}, u32[]{:S(2)}, u32[]{:S(2)}) collective-permute-start(bf16[80,1792]{1,0:T(8,128)(2,1)S(1)} %copy-done.9), channel_id=1, source_target_pairs={{0,16},{8,24},{16,0},{24,8},{1,17},{9,25},{17,1},{25,9},{2,18},{10... | collective-permute-start | bytes 860168 | tf_op jit(solution)/shard_map/ppermute | solution.py:375
  13.9 1.3 collective-permute-start.3
  15.3 9.1 %all-to-all-start = ((bf16[32,8,1920]{2,1,0:T(8,128)(2,1)}), bf16[32,8,1920]{2,1,0:T(8,128)(2,1)}, u32[]{:S(2)}, u32[]{:S(2)}) async-start(bf16[32,8,1920]{2,1,0:T(8,128)(2,1)} %bitcast.28), calls=%async_computation | async-start | bytes 1966080 | tf_op jit(solution)/shard_map/all_to_all | solution.py:388
  24.4 0.1 broadcast_multiply_fusion.1
  24.5 0.1 copy.21
  24.6 1.2 fusion.8
  25.8 7.4 %attention.2 = (bf16[256,1280]{1,0:T(8,128)(2,1)}, bf16[256,1280]{1,0:T(8,128)(2,1)}, bf16[256,1280]{1,0:T(8,128)(2,1)}) custom-call(bf16[256,1280]{1,0:T(8,128)(2,1)} %q_ref.1, bf16[256,1280]{1,0:T(8,128)(2,1)} %k_ref.3, bf16[256,1280]{1,0:T(8,128)(2,1)} %v_ref.3, bf16[256,1280]{1,0:T(8,128)(2,1)} %g_ref.3, f32[256,40]{1,0:T(8,128)} %get-tuple-element.52.cos_ref, ...), custom_call_target="tpu_custom_call" | custom-call | flops 1677721600 | bytes 2949120 | tf_op jit(solution)/shard_map/attention/pallas_call | solution.py:343
  33.2 7.4 %attention.3 = (bf16[256,1280]{1,0:T(8,128)(2,1)}, bf16[256,1280]{1,0:T(8,128)(2,1)}, bf16[256,1280]{1,0:T(8,128)(2,1)}) custom-call(bf16[256,1280]{1,0:T(8,128)(2,1)} %q_ref.1, bf16[256,1280]{1,0:T(8,128)(2,1)} %k_ref.3, bf16[256,1280]{1,0:T(8,128)(2,1)} %v_ref.3, ...), custom_call_target="tpu_custom_call", output_to_operand_aliasing={{0}: (6, {}), {1}: (7, {}), {2}: (8, {})} | custom-call | flops 1677721600 | bytes 2949120 | tf_op jit(solution)/shard_map/attention/pallas_call | solution.py:343
  40.6 2.5 %constant_dynamic-slice_fusion.1 = bf16[2,1280,256]{2,1,0:T(8,128)(2,1)} fusion(bf16[2,2560,256]{2,1,0:T(8,128)(2,1)} %collective-permute-done.6.mine, s32[]{:T(128)S(6)} %select_n.126), kind=kLoop, calls=%fused_computation.29 | loop fusion | bytes 2621444 | tf_op jit(solution)/shard_map/dynamic_slice | solution.py:406
  43.2 1.2 collective-permute-start.8
  44.4 5.7 %all-to-all-done = bf16[32,8,1920]{2,1,0:T(8,128)(2,1)} async-done(((bf16[32,8,1920]{2,1,0:T(8,128)(2,1)}), bf16[32,8,1920]{2,1,0:T(8,128)(2,1)}, u32[]{:S(2)}, u32[]{:S(2)}) %all-to-all-start) | async-done | bytes 983072 | tf_op jit(solution)/shard_map/all_to_all | solution.py:388
  50.1 1.9 %land.1 = (bf16[256,1792]{1,0:T(8,128)(2,1)S(1)}, bf16[8,224,256]{2,1,0:T(8,128)(2,1)S(1)}) custom-call(bf16[256,1920]{1,0:T(8,128)(2,1)} %bitcast.5.inc_ref), custom_call_target="tpu_custom_call" | custom-call | flops 234881024 | bytes 2752512 | tf_op jit(solution)/shard_map/land/pallas_call | solution.py:96
  52.0 0.9 copy-done.2
  52.9 0.9 copy-done.3
  53.8 6.0 %all-to-all-start.1 = ((bf16[8,224,256]{2,1,0:T(8,128)(2,1)}), bf16[8,224,256]{2,1,0:T(8,128)(2,1)S(1)}, u32[]{:S(2)}, u32[]{:S(2)}) async-start(bf16[8,224,256]{2,1,0:T(8,128)(2,1)} %copy-done.3), calls=%async_computation.1 | async-start | bytes 1835008 | tf_op jit(solution)/shard_map/all_to_all | solution.py:410
  59.8 2.4 %pad_maximum_fusion.1.refs_0_ = bf16[4,80,1792]{2,1,0:T(8,128)(2,1)} fusion(bf16[1,80,1792]{2,1,0:T(8,128)(2,1)} %bitcast.9, bf16[1,80,1792]{2,1,0:T(8,128)(2,1)} %bitcast.8, bf16[1,80,1792]{2,1,0:T(8,128)(2,1)} %bitcast.31, bf16[1,80,1792]{2,1,0:T(8,128)(2,1)} %bitcast.30), kind=kLoop, calls=%fused_computation.1 | loop fusion | flops 1720320 | bytes 2293760 | tf_op jit(solution)/shard_map/stack | solution.py:429
  62.3 1.5 %collective-permute-start.4 = (bf16[4,80,1792]{2,1,0:T(8,128)(2,1)}, bf16[4,80,1792]{2,1,0:T(8,128)(2,1)}, u32[]{:S(2)}, u32[]{:S(2)}) collective-permute-start(bf16[4,80,1792]{2,1,0:T(8,128)(2,1)} %pad_maximum_fusion.1.refs_0_), channel_id=1, source_target_pairs={{0,1},{1,2},{2,3},{3,4},{4,5},{5,6},{6,7},{7,0},{32,39},{33,32},{3... | collective-permute-start | bytes 3440648 | tf_op jit(solution)/shard_map/ppermute | solution.py:382
  63.8 9.1 %all-to-all-done.1.cols_ref = bf16[8,224,256]{2,1,0:T(8,128)(2,1)S(1)} async-done(((bf16[8,224,256]{2,1,0:T(8,128)(2,1)}), bf16[8,224,256]{2,1,0:T(8,128)(2,1)S(1)}, u32[]{:S(2)}, u32[]{:S(2)}) %all-to-all-start.1) | async-done | bytes 917536 | tf_op jit(solution)/shard_map/all_to_all | solution.py:410
  73.0 6.7 %collective-permute-done.4.refs_1_ = bf16[4,80,1792]{2,1,0:T(8,128)(2,1)} collective-permute-done((bf16[4,80,1792]{2,1,0:T(8,128)(2,1)}, bf16[4,80,1792]{2,1,0:T(8,128)(2,1)}, u32[]{:S(2)}, u32[]{:S(2)}) %collective-permute-start.4) | collective-permute-done | bytes 1146912 | tf_op jit(solution)/shard_map/ppermute | solution.py:382
  79.6 0.3 collective-permute-start.5
  80.0 0.1 stack.115.idx_ref
  80.1 8.5 %weight.1 = (f32[320,224]{1,0:T(8,128)S(1)}, f32[320,224]{1,0:T(8,128)S(1)}, f32[2,320,224]{2,1,0:T(8,128)}, f32[2,320,224]{2,1,0:T(8,128)}, f32[2,320,224]{2,1,0:T(8,128)S(1)}) custom-call(s32[16]{0:T(128)S(1)} %stack.115.idx_ref, bf16[8,224,256]{2,1,0:T(8,128)(2,1)S(1)} %all-to-all-done.1.cols_ref, bf16[2,2560,256]{2,1,0:T(8,128)(2,1)S(1)} %pad_maximum_fusion.own, ...), custom_call_target="tpu_custom_call" | custom-call | flops 2348810240 | bytes 12779520 | tf_op jit(solution)/shard_map/weight/pallas_call | solution.py:224
  88.6 0.6 collective-permute-start.10
  89.2 2.6 %collective-permute-start.11 = (f32[320,224]{1,0:T(8,128)S(1)}, f32[320,224]{1,0:T(8,128)S(1)}, u32[]{:S(2)}, u32[]{:S(2)}) collective-permute-start(f32[320,224]{1,0:T(8,128)S(1)} %get-tuple-element.45), channel_id=1, source_target_pairs={{0,24},{8,0},{16,8},{24,16},{1,25},{9,1},{17,9},{25,17},{2,26},{10... | collective-permute-start | bytes 860168 | tf_op jit(solution)/shard_map/ppermute | solution.py:375
  91.8 5.2 %collective-permute-done.5.refs_2_ = bf16[4,80,1792]{2,1,0:T(8,128)(2,1)} collective-permute-done((bf16[4,80,1792]{2,1,0:T(8,128)(2,1)}, bf16[4,80,1792]{2,1,0:T(8,128)(2,1)}, u32[]{:S(2)}, u32[]{:S(2)}) %collective-permute-start.5) | collective-permute-done | bytes 1146912 | tf_op jit(solution)/shard_map/ppermute | solution.py:382
  97.0 1.4 collective-permute-done.10.add_ref
  98.4 0.6 collective-permute-start.12
  98.9 1.7 %add.214 = f32[2,320,224]{2,1,0:T(8,128)} custom-call(f32[2,320,224]{2,1,0:T(8,128)} %get-tuple-element.48.rows_ref, f32[320,224]{1,0:T(8,128)S(1)} %collective-permute-done.10.add_ref), custom_call_target="tpu_custom_call", output_to_operand_aliasing={{}: (0, {})} | custom-call | flops 71680 | bytes 860160 | tf_op jit(solution)/shard_map/add/pallas_call | solution.py:246
  100.7 0.5 collective-permute-start.18
  101.2 1.8 %add.215 = f32[2,320,224]{2,1,0:T(8,128)} custom-call(f32[2,320,224]{2,1,0:T(8,128)} %get-tuple-element.49.rows_ref, f32[320,224]{1,0:T(8,128)S(1)} %collective-permute-done.11.add_ref), custom_call_target="tpu_custom_call", output_to_operand_aliasing={{}: (0, {})} | custom-call | flops 71680 | bytes 860160 | tf_op jit(solution)/shard_map/add/pallas_call | solution.py:246
  103.0 2.7 %collective-permute-start.19 = (f32[2,320,224]{2,1,0:T(8,128)}, f32[2,320,224]{2,1,0:T(8,128)S(1)}, u32[]{:S(2)}, u32[]{:S(2)}) collective-permute-start(f32[2,320,224]{2,1,0:T(8,128)} %add.215), channel_id=1, source_target_pairs={{0,24},{8,0},{16,8},{24,16},{1,25},{9,1},{17,9},{25,17},{2,26},{10... | collective-permute-start | bytes 1720328 | tf_op jit(solution)/shard_map/ppermute | solution.py:375
  105.7 10.0 %collective-permute-done.12.refs_3_ = bf16[4,80,1792]{2,1,0:T(8,128)(2,1)S(1)} collective-permute-done((bf16[4,80,1792]{2,1,0:T(8,128)(2,1)}, bf16[4,80,1792]{2,1,0:T(8,128)(2,1)S(1)}, u32[]{:S(2)}, u32[]{:S(2)}) %collective-permute-start.12) | collective-permute-done | bytes 1146912 | tf_op jit(solution)/shard_map/ppermute | solution.py:382
  115.7 0.9 constant_dynamic-slice_fusion
  116.6 0.5 collective-permute-start.15
  117.1 1.1 collective-permute-done.19
  118.2 1.0 add_add_fusion
  119.2 6.0 %all-to-all-start.2 = ((f32[8,80,224]{2,1,0:T(8,128)}), f32[8,80,224]{2,1,0:T(8,128)S(1)}, u32[]{:S(2)}, u32[]{:S(2)}) async-start(f32[8,80,224]{2,1,0:T(8,128)} %bitcast.26), calls=%async_computation.2 | async-start | bytes 1310720 | tf_op jit(solution)/shard_map/all_to_all | solution.py:448
  125.2 2.6 %collective-permute-done.13.refs_4_ = bf16[2,80,1792]{2,1,0:T(8,128)(2,1)} collective-permute-done((bf16[2,80,1792]{2,1,0:T(8,128)(2,1)}, bf16[2,80,1792]{2,1,0:T(8,128)(2,1)}, u32[]{:S(2)}, u32[]{:S(2)}) %collective-permute-start.13) | collective-permute-done | bytes 573472 | tf_op jit(solution)/shard_map/ppermute | solution.py:382
  127.8 0.1 broadcast_in_dim.76
  127.9 0.1 broadcast_in_dim.77
  128.0 0.1 broadcast_in_dim.86
  128.0 0.1 broadcast_in_dim.87
  128.1 0.1 broadcast_in_dim.80
  128.2 0.1 broadcast_in_dim.81
  128.3 0.1 broadcast_in_dim.79
  128.4 0.1 broadcast_in_dim.83
  128.5 0.1 add.162
  128.6 0.1 broadcast_in_dim.75
  128.7 0.5 fusion.2.at_ref
  129.3 0.7 collective-permute-done.17.refs_8_
  130.0 0.8 copy-done.8
  130.8 10.3 %hidden.1 = bf16[256,2560]{1,0:T(8,128)(2,1)} custom-call(s32[32]{0:T(128)} %fusion.2.at_ref, bf16[256,1792]{1,0:T(8,128)(2,1)} %copy-done.2, bf16[256,2560]{1,0:T(8,128)(2,1)} %pre_ref.2, bf16[4,80,1792]{2,1,0:T(8,128)(2,1)} %pad_maximum_fusion.1.refs_0_, bf16[4,80,1792]{2,1,0:T(8,128)(2,1)} %collective-permute-done.4.refs_1_, ...), custom_call_target="tpu_custom_call" | custom-call | flops 2348810240 | bytes 11796480 | tf_op jit(solution)/shard_map/hidden/pallas_call | solution.py:160
  141.1 4.4 %all-to-all-done.2 = f32[8,80,224]{2,1,0:T(8,128)S(1)} async-done(((f32[8,80,224]{2,1,0:T(8,128)}), f32[8,80,224]{2,1,0:T(8,128)S(1)}, u32[]{:S(2)}, u32[]{:S(2)}) %all-to-all-start.2) | async-done | bytes 573472 | tf_op jit(solution)/shard_map/all_to_all | solution.py:448
  145.5 0.7 reduce_sum.9
  (49 shorter events, 0.2 us)
Async XLA Ops:
  0.6 2.7 %copy-start = (bf16[256,2560]{1,0:T(8,128)(2,1)S(1)}, bf16[256,2560]{1,0:T(8,128)(2,1)}, u32[]{:S(2)}) copy-start(bf16[256,2560]{1,0:T(8,128)(2,1)} %pre_ref.2) | copy-start | bytes 3932164
  1.5 1.0 copy-start.6
  3.4 4.2 %copy-start.1 = (bf16[256,1920]{1,0:T(8,128)(2,1)}, bf16[256,1920]{1,0:T(8,128)(2,1)S(1)}, u32[]{:S(2)}) copy-start(bf16[256,1920]{1,0:T(8,128)(2,1)S(1)} %pack.1) | copy-start | bytes 2949124
  4.5 3.1 %collective-permute-start = (bf16[2560,256]{1,0:T(8,128)(2,1)S(1)}, bf16[2560,256]{1,0:T(8,128)(2,1)S(1)}, u32[]{:S(2)}, u32[]{:S(2)}) collective-permute-start(bf16[2560,256]{1,0:T(8,128)(2,1)S(1)} %act.1), channel_id=1, source_target_pairs={{0,32},{32,0},{1,33},{33,1},{2,34},{34,2},{3,35},{35,3},{4,36},{36... | collective-permute-start | bytes 3932168 | tf_op jit(solution)/shard_map/ppermute | solution.py:375
  7.6 1.8 %copy-start.9 = (bf16[80,1792]{1,0:T(8,128)(2,1)S(1)}, bf16[80,1792]{1,0:T(8,128)(2,1)}, u32[]{:S(2)}) copy-start(bf16[80,1792]{1,0:T(8,128)(2,1)} %param.12) | copy-start | bytes 860164
  7.8 16.5 %copy-start.11 = (s32[2,256]{1,0:T(2,128)S(1)}, s32[2,256]{1,0:T(2,128)}, u32[]{:S(2)}) copy-start(s32[2,256]{1,0:T(2,128)} %param.17) | copy-start | bytes 6148
  7.9 32.8 %collective-permute-start.6 = (bf16[2,2560,256]{2,1,0:T(8,128)(2,1)S(1)}, bf16[2,2560,256]{2,1,0:T(8,128)(2,1)}, u32[]{:S(2)}, u32[]{:S(2)}) collective-permute-start(bf16[2,2560,256]{2,1,0:T(8,128)(2,1)S(1)} %pad_maximum_fusion.own), channel_id=1, source_target_pairs={{0,64},{64,128},{128,192},{192,0},{32,224},{96,32},{160,96},{224,1... | collective-permute-start | bytes 7864328 | tf_op jit(solution)/shard_map/ppermute | solution.py:381
  9.4 31.2 %collective-permute-start.1 = (bf16[80,1792]{1,0:T(8,128)(2,1)S(1)}, bf16[80,1792]{1,0:T(8,128)(2,1)S(1)}, u32[]{:S(2)}, u32[]{:S(2)}) collective-permute-start(bf16[80,1792]{1,0:T(8,128)(2,1)S(1)} %copy-done.9), channel_id=1, source_target_pairs={{0,8},{8,16},{16,24},{24,0},{1,9},{9,17},{17,25},{25,1},{2,10},{10... | collective-permute-start | bytes 860168 | tf_op jit(solution)/shard_map/ppermute | solution.py:375
  11.0 29.6 %collective-permute-start.2 = (bf16[80,1792]{1,0:T(8,128)(2,1)S(1)}, bf16[80,1792]{1,0:T(8,128)(2,1)}, u32[]{:S(2)}, u32[]{:S(2)}) collective-permute-start(bf16[80,1792]{1,0:T(8,128)(2,1)S(1)} %copy-done.9), channel_id=1, source_target_pairs={{0,16},{8,24},{16,0},{24,8},{1,17},{9,25},{17,1},{25,9},{2,18},{10... | collective-permute-start | bytes 860168 | tf_op jit(solution)/shard_map/ppermute | solution.py:375
  13.9 26.7 %collective-permute-start.3 = (bf16[80,1792]{1,0:T(8,128)(2,1)S(1)}, bf16[80,1792]{1,0:T(8,128)(2,1)}, u32[]{:S(2)}, u32[]{:S(2)}) collective-permute-start(bf16[80,1792]{1,0:T(8,128)(2,1)S(1)} %copy-done.9), channel_id=1, source_target_pairs={{0,24},{8,0},{16,8},{24,16},{1,25},{9,1},{17,9},{25,17},{2,26},{10... | collective-permute-start | bytes 860168 | tf_op jit(solution)/shard_map/ppermute | solution.py:375
  15.3 34.8 %all-to-all-start = ((bf16[32,8,1920]{2,1,0:T(8,128)(2,1)}), bf16[32,8,1920]{2,1,0:T(8,128)(2,1)}, u32[]{:S(2)}, u32[]{:S(2)}) async-start(bf16[32,8,1920]{2,1,0:T(8,128)(2,1)} %bitcast.28), calls=%async_computation | async-start | bytes 1966080 | tf_op jit(solution)/shard_map/all_to_all | solution.py:388
  40.6 2.6 %copy-start.10 = (bf16[80,1792]{1,0:T(8,128)(2,1)}, bf16[80,1792]{1,0:T(8,128)(2,1)S(1)}, u32[]{:S(2)}) copy-start(bf16[80,1792]{1,0:T(8,128)(2,1)S(1)} %collective-permute-done.1) | copy-start | bytes 860164
  43.2 29.8 %collective-permute-start.8 = (bf16[2,1280,256]{2,1,0:T(8,128)(2,1)}, bf16[2,1280,256]{2,1,0:T(8,128)(2,1)}, u32[]{:S(2)}, u32[]{:S(2)}) collective-permute-start(bf16[2,1280,256]{2,1,0:T(8,128)(2,1)} %constant_dynamic-slice_fusion.1), channel_id=1, source_target_pairs={{0,64},{64,128},{128,192},{192,0},{32,224},{96,32},{160,96},{224,1... | collective-permute-start | bytes 3932168 | tf_op jit(solution)/shard_map/ppermute | solution.py:381
  44.4 35.7 %collective-permute-start.7 = (bf16[2,2560,256]{2,1,0:T(8,128)(2,1)}, bf16[2,2560,256]{2,1,0:T(8,128)(2,1)}, u32[]{:S(2)}, u32[]{:S(2)}) collective-permute-start(bf16[2,2560,256]{2,1,0:T(8,128)(2,1)} %collective-permute-done.6.mine), channel_id=1, source_target_pairs={{0,32},{32,0},{1,33},{33,1},{2,34},{34,2},{3,35},{35,3},{4,36},{36... | collective-permute-start | bytes 7864328 | tf_op jit(solution)/shard_map/ppermute | solution.py:375
  52.0 0.9 copy-start.2
  52.9 0.9 copy-start.3
  53.8 19.1 %all-to-all-start.1 = ((bf16[8,224,256]{2,1,0:T(8,128)(2,1)}), bf16[8,224,256]{2,1,0:T(8,128)(2,1)S(1)}, u32[]{:S(2)}, u32[]{:S(2)}) async-start(bf16[8,224,256]{2,1,0:T(8,128)(2,1)} %copy-done.3), calls=%async_computation.1 | async-start | bytes 1835008 | tf_op jit(solution)/shard_map/all_to_all | solution.py:410
  62.3 17.4 %collective-permute-start.4 = (bf16[4,80,1792]{2,1,0:T(8,128)(2,1)}, bf16[4,80,1792]{2,1,0:T(8,128)(2,1)}, u32[]{:S(2)}, u32[]{:S(2)}) collective-permute-start(bf16[4,80,1792]{2,1,0:T(8,128)(2,1)} %pad_maximum_fusion.1.refs_0_), channel_id=1, source_target_pairs={{0,1},{1,2},{2,3},{3,4},{4,5},{5,6},{6,7},{7,0},{32,39},{33,32},{3... | collective-permute-start | bytes 3440648 | tf_op jit(solution)/shard_map/ppermute | solution.py:382
  73.0 7.1 %collective-permute-start.9 = (bf16[2,1280,256]{2,1,0:T(8,128)(2,1)}, bf16[2,1280,256]{2,1,0:T(8,128)(2,1)}, u32[]{:S(2)}, u32[]{:S(2)}) collective-permute-start(bf16[2,1280,256]{2,1,0:T(8,128)(2,1)} %collective-permute-done.8.mine_half), channel_id=1, source_target_pairs={{0,32},{32,0},{1,33},{33,1},{2,34},{34,2},{3,35},{35,3},{4,36},{36... | collective-permute-start | bytes 3932168 | tf_op jit(solution)/shard_map/ppermute | solution.py:375
  79.6 17.4 %collective-permute-start.5 = (bf16[4,80,1792]{2,1,0:T(8,128)(2,1)}, bf16[4,80,1792]{2,1,0:T(8,128)(2,1)}, u32[]{:S(2)}, u32[]{:S(2)}) collective-permute-start(bf16[4,80,1792]{2,1,0:T(8,128)(2,1)} %collective-permute-done.4.refs_1_), channel_id=1, source_target_pairs={{0,1},{1,2},{2,3},{3,4},{4,5},{5,6},{6,7},{7,0},{32,39},{33,32},{3... | collective-permute-start | bytes 3440648 | tf_op jit(solution)/shard_map/ppermute | solution.py:382
  88.6 14.4 %copy-start.4 = (f32[2,320,224]{2,1,0:T(8,128)}, f32[2,320,224]{2,1,0:T(8,128)S(1)}, u32[]{:S(2)}) copy-start(f32[2,320,224]{2,1,0:T(8,128)S(1)} %get-tuple-element.47) | copy-start | bytes 1720324
  88.6 9.8 %collective-permute-start.10 = (f32[320,224]{1,0:T(8,128)S(1)}, f32[320,224]{1,0:T(8,128)S(1)}, u32[]{:S(2)}, u32[]{:S(2)}) collective-permute-start(f32[320,224]{1,0:T(8,128)S(1)} %get-tuple-element.44), channel_id=1, source_target_pairs={{0,8},{8,16},{16,24},{24,0},{1,9},{9,17},{17,25},{25,1},{2,10},{10... | collective-permute-start | bytes 860168 | tf_op jit(solution)/shard_map/ppermute | solution.py:375
  89.2 9.1 %collective-permute-start.11 = (f32[320,224]{1,0:T(8,128)S(1)}, f32[320,224]{1,0:T(8,128)S(1)}, u32[]{:S(2)}, u32[]{:S(2)}) collective-permute-start(f32[320,224]{1,0:T(8,128)S(1)} %get-tuple-element.45), channel_id=1, source_target_pairs={{0,24},{8,0},{16,8},{24,16},{1,25},{9,1},{17,9},{25,17},{2,26},{10... | collective-permute-start | bytes 860168 | tf_op jit(solution)/shard_map/ppermute | solution.py:375
  98.4 17.3 %collective-permute-start.12 = (bf16[4,80,1792]{2,1,0:T(8,128)(2,1)}, bf16[4,80,1792]{2,1,0:T(8,128)(2,1)S(1)}, u32[]{:S(2)}, u32[]{:S(2)}) collective-permute-start(bf16[4,80,1792]{2,1,0:T(8,128)(2,1)} %collective-permute-done.5.refs_2_), channel_id=1, source_target_pairs={{0,1},{1,2},{2,3},{3,4},{4,5},{5,6},{6,7},{7,0},{32,39},{33,32},{3... | collective-permute-start | bytes 3440648 | tf_op jit(solution)/shard_map/ppermute | solution.py:382
  100.7 16.4 %collective-permute-start.18 = (f32[2,320,224]{2,1,0:T(8,128)}, f32[2,320,224]{2,1,0:T(8,128)S(1)}, u32[]{:S(2)}, u32[]{:S(2)}) collective-permute-start(f32[2,320,224]{2,1,0:T(8,128)} %add.214), channel_id=1, source_target_pairs={{0,8},{8,16},{16,24},{24,0},{1,9},{9,17},{17,25},{25,1},{2,10},{10... | collective-permute-start | bytes 1720328 | tf_op jit(solution)/shard_map/ppermute | solution.py:375
  103.0 15.2 %collective-permute-start.19 = (f32[2,320,224]{2,1,0:T(8,128)}, f32[2,320,224]{2,1,0:T(8,128)S(1)}, u32[]{:S(2)}, u32[]{:S(2)}) collective-permute-start(f32[2,320,224]{2,1,0:T(8,128)} %add.215), channel_id=1, source_target_pairs={{0,24},{8,0},{16,8},{24,16},{1,25},{9,1},{17,9},{25,17},{2,26},{10... | collective-permute-start | bytes 1720328 | tf_op jit(solution)/shard_map/ppermute | solution.py:375
  105.7 12.5 %copy-start.5 = (f32[2,320,224]{2,1,0:T(8,128)S(1)}, f32[2,320,224]{2,1,0:T(8,128)}, u32[]{:S(2)}) copy-start(f32[2,320,224]{2,1,0:T(8,128)} %copy-done.4) | copy-start | bytes 1720324
  115.7 3.5 %copy-start.7 = (bf16[4,80,1792]{2,1,0:T(8,128)(2,1)}, bf16[4,80,1792]{2,1,0:T(8,128)(2,1)S(1)}, u32[]{:S(2)}) copy-start(bf16[4,80,1792]{2,1,0:T(8,128)(2,1)S(1)} %collective-permute-done.12.refs_3_) | copy-start | bytes 3440644
  116.6 11.2 %collective-permute-start.13 = (bf16[2,80,1792]{2,1,0:T(8,128)(2,1)}, bf16[2,80,1792]{2,1,0:T(8,128)(2,1)}, u32[]{:S(2)}, u32[]{:S(2)}) collective-permute-start(bf16[2,80,1792]{2,1,0:T(8,128)(2,1)} %constant_dynamic-slice_fusion), channel_id=1, source_target_pairs={{0,1},{1,2},{2,3},{3,4},{4,5},{5,6},{6,7},{7,0},{32,39},{33,32},{3... | collective-permute-start | bytes 1720328 | tf_op jit(solution)/shard_map/ppermute | solution.py:382
  116.6 12.7 %collective-permute-start.14 = (bf16[4,80,1792]{2,1,0:T(8,128)(2,1)}, bf16[4,80,1792]{2,1,0:T(8,128)(2,1)}, u32[]{:S(2)}, u32[]{:S(2)}) collective-permute-start(bf16[4,80,1792]{2,1,0:T(8,128)(2,1)} %collective-permute-done.4.refs_1_), channel_id=1, source_target_pairs={{0,32},{32,0},{1,33},{33,1},{2,34},{34,2},{3,35},{35,3},{4,36},{36... | collective-permute-start | bytes 3440648 | tf_op jit(solution)/shard_map/ppermute | solution.py:375
  116.6 12.7 %collective-permute-start.15 = (bf16[4,80,1792]{2,1,0:T(8,128)(2,1)}, bf16[4,80,1792]{2,1,0:T(8,128)(2,1)}, u32[]{:S(2)}, u32[]{:S(2)}) collective-permute-start(bf16[4,80,1792]{2,1,0:T(8,128)(2,1)} %collective-permute-done.5.refs_2_), channel_id=1, source_target_pairs={{0,32},{32,0},{1,33},{33,1},{2,34},{34,2},{3,35},{35,3},{4,36},{36... | collective-permute-start | bytes 3440648 | tf_op jit(solution)/shard_map/ppermute | solution.py:375
  117.1 12.9 %collective-permute-start.16 = (bf16[4,80,1792]{2,1,0:T(8,128)(2,1)S(1)}, bf16[4,80,1792]{2,1,0:T(8,128)(2,1)}, u32[]{:S(2)}, u32[]{:S(2)}) collective-permute-start(bf16[4,80,1792]{2,1,0:T(8,128)(2,1)S(1)} %collective-permute-done.12.refs_3_), channel_id=1, source_target_pairs={{0,32},{32,0},{1,33},{33,1},{2,34},{34,2},{3,35},{35,3},{4,36},{36... | collective-permute-start | bytes 3440648 | tf_op jit(solution)/shard_map/ppermute | solution.py:375
  119.2 26.4 %all-to-all-start.2 = ((f32[8,80,224]{2,1,0:T(8,128)}), f32[8,80,224]{2,1,0:T(8,128)S(1)}, u32[]{:S(2)}, u32[]{:S(2)}) async-start(f32[8,80,224]{2,1,0:T(8,128)} %bitcast.26), calls=%async_computation.2 | async-start | bytes 1310720 | tf_op jit(solution)/shard_map/all_to_all | solution.py:448
  127.8 2.2 %collective-permute-start.17 = (bf16[2,80,1792]{2,1,0:T(8,128)(2,1)}, bf16[2,80,1792]{2,1,0:T(8,128)(2,1)S(1)}, u32[]{:S(2)}, u32[]{:S(2)}) collective-permute-start(bf16[2,80,1792]{2,1,0:T(8,128)(2,1)} %collective-permute-done.13.refs_4_), channel_id=1, source_target_pairs={{0,32},{32,0},{1,33},{33,1},{2,34},{34,2},{3,35},{35,3},{4,36},{36... | collective-permute-start | bytes 1720328 | tf_op jit(solution)/shard_map/ppermute | solution.py:375
  130.0 0.8 copy-start.8

commit v2 on v1

--- a/solution.py
+++ b/solution.py
@@ -99,7 +99,7 @@
             jax.ShapeDtypeStruct((slots, width), BF16),
             jax.ShapeDtypeStruct((parts, width // parts, slots), BF16),
         ),
-        compiler_params=params(),
+        compiler_params=params(58),
         cost_estimate=cost(2 * slots * slots * width, 6 * slots * width),
         name="land",
     )(incoming)
@@ -181,7 +181,8 @@
 
 
 def weight_kernel(scale, idx_ref, cols_ref, own, mine, other, mine_half, other_half, *refs):
-    outs, cols = refs[:5], refs[5]
+    *outs, cols = refs
+    count = pl.num_programs(0)
     step = pl.program_id(0)
     slots = own.shape[2]
 
@@ -190,70 +191,68 @@
         for j in range(8):
             cols[j * slots : (j + 1) * slots] = cols_ref[idx_ref[j]].astype(F32).T.astype(BF16)
 
-    ours = idx_ref[12 + step] == 1
+    ours = idx_ref[8 + count + step] == 1
     across = [jnp.where(ours, mine_half[i], other_half[1 - i]) for i in (0, 1)]
     rows = [own[0], own[1], mine[0], mine[1], other[0], other[1], *across]
     total = mm(jnp.concatenate(rows, axis=1), cols[...]) * scale
 
-    @pl.when(step == 0)
-    def _():
-        cut = total.shape[0] // 2
-        outs[0][...] = total[:cut]
-        outs[1][...] = total[cut:]
-
-    for q in range(3):
-
-        @pl.when(step == q + 1)
-        def _(q=q):
-            cut = total.shape[0] // 2
-            outs[2 + q][0] = total[:cut]
-            outs[2 + q][1] = total[cut:]
+    cut = total.shape[0] // 2
+    for q, out in enumerate(outs):
+
+        @pl.when(step == q)
+        def _(out=out):
+            out[0] = total[:cut]
+            out[1] = total[cut:]
 
 
 def weight_rows(idx, cols, own, mine, other, mine_half, other_half, scale):
     _, hid, slots = own.shape
     part = cols.shape[1]
     block = hid // 4
+    count = (idx.shape[0] - 8) // 2
 
     def whole(shape):
         return pl.BlockSpec(shape, lambda i, s: (0,) * len(shape))
 
     full = pl.BlockSpec((2, block, slots), lambda i, s: (0, s[8 + i], 0))
     half = pl.BlockSpec((2, block, slots), lambda i, s: (0, s[8 + i] % 2, 0))
-    shapes = [(block // 2, part)] * 2 + [(2, block // 2, part)] * 3
+    shapes = [(2, block // 2, part)] * count
     return pl.pallas_call(
         functools.partial(weight_kernel, scale),
         grid_spec=pltpu.PrefetchScalarGridSpec(
             num_scalar_prefetch=1,
-            grid=(4,),
+            grid=(count,),
             in_specs=[whole(cols.shape), full, full, full, half, half],
             out_specs=[whole(shape) for shape in shapes],
             scratch_shapes=[pltpu.VMEM((8 * slots, part), BF16)],
         ),
         out_shape=[jax.ShapeDtypeStruct(shape, F32) for shape in shapes],
         compiler_params=params(),
-        cost_estimate=cost(2 * hid * slots * 8 * part, 2 * hid * slots * 8 + 4 * hid * part),
+        cost_estimate=cost(2 * count * block * slots * 8 * part, 16 * count * block * slots),
         name="weight",
     )(idx, cols, own, mine, other, mine_half, other_half)
 
 
-def add_kernel(rows_ref, add_ref, out_ref):
-    out_ref[0] = rows_ref[0] + add_ref[...]
-
-
-def added(rows, addend, at):
-    block = pl.BlockSpec((1, *addend.shape), lambda i: (at, 0, 0))
+def add_kernel(above_ref, below_ref, low_ref, high_ref, above_out, below_out):
+    above_out[0] = above_ref[0] + low_ref[...]
+    below_out[0] = below_ref[0] + high_ref[...]
+
+
+def added(above, below, low, high):
+    whole = pl.BlockSpec(low.shape, lambda i: (0, 0))
+    first = pl.BlockSpec((1, *low.shape), lambda i: (0, 0, 0))
+    second = pl.BlockSpec((1, *low.shape), lambda i: (1, 0, 0))
     return pl.pallas_call(
         add_kernel,
         grid=(1,),
-        in_specs=[block, pl.BlockSpec(addend.shape, lambda i: (0, 0))],
-        out_specs=block,
-        out_shape=jax.ShapeDtypeStruct(rows.shape, rows.dtype),
-        input_output_aliases={0: 0},
+        in_specs=[first, second, whole, whole],
+        out_specs=[first, second],
+        out_shape=[jax.ShapeDtypeStruct(above.shape, above.dtype)] * 2,
+        input_output_aliases={0: 0, 1: 1},
         compiler_params=params(),
-        cost_estimate=cost(addend.size, 12 * addend.size),
+        cost_estimate=cost(2 * low.size, 24 * low.size),
         name="add",
-    )(rows, addend)
+    )(above, below, low, high)
 
 
 def attention_kernel(q_ref, k_ref, v_ref, g_ref, cos_ref, sin_ref, *refs):
@@ -415,21 +414,24 @@
     places = []
     for there, core in ((x, k), (before, k), (behind, 1 - k), ((x + 2) % xs, k)):
         places += [2 * there + core, 2 * there + 1 - core]
-    quarters = [(y + dy) % ys for dy in (2, 1, 3, 0)]
-    ours = [(q < 2) == (k == 0) for q in quarters]
     factor = (rows_here * owners * replicas) ** (-0.5)
-    idx = numbers(*places, *quarters, *ours)
-    top, bottom, above, below, here = weight_rows(
-        idx, cols, own, mine, other, mine_half, other_half, factor
-    )
-    from_below, from_above = hop(top, "y", 1), hop(bottom, "y", -1)
-    above = hop(added(above, from_below, 0), "y", 1)
-    below = hop(added(below, from_above, 1), "y", -1)
+
+    def rows_of(steps, *earlier):
+        quarters = [(y + dy) % ys for dy in steps]
+        ours = [(q < 2) == (k == 0) for q in quarters]
+        idx = after(numbers(*places, *quarters, *ours), *earlier)
+        return weight_rows(idx, cols, own, mine, other, mine_half, other_half, factor)
+
+    (across,) = rows_of((2,))
+    from_below, from_above = hop(across[0], "y", 1), hop(across[1], "y", -1)
+    above, below, here = rows_of((1, 3, 0), across)
+    above, below = added(above, below, from_below, from_above)
+    above, below = hop(above, "y", 1), hop(below, "y", -1)
 
     line = jnp.stack([line, *beside])
     ones = [apart(after(line, slotted), "z")]
     ones.append(apart(ones[0], "z"))
-    ones.append(apart(after(ones[1], from_below, from_above), "z"))
+    ones.append(apart(after(ones[1], from_below, from_above, here), "z"))
     last = lax.dynamic_slice_in_dim(ones[2], k * (ys // 2), ys // 2, axis=0)
     ones.append(apart(last, "z"))
     lines = [line, *ones, *(hop(part, "k", 1) for part in ones)]

time: 148 us -> 146 us (0.986)
  Pallas kernels: 41 us -> 43.1 us
  starting transfers between devices: 39.2 us -> 37.2 us
  waiting for transfers between devices: 49.9 us -> 47.9 us
    ppermute x4, waiting for transfers between devices: 24.4 us -> 29.3 us  [apart(): lax.ppermute(v, ('k', axis), [(n * core + i, n * core + j) for core, i, j...]
    all_to_all x1, waiting for transfers between devices: 4.39 us -> 0.01 us  [shards(): lax.all_to_all(pieces, 'z', split_axis=0, concat_axis=0, tiled=True)]
    ppermute x14, waiting for transfers between devices: 6.23 us -> 3.79 us  [hop(): return lax.ppermute(v, axis, shifted(lax.axis_size(axis), by))]
    pallas_call x1 -> x2, Pallas kernels: 8.52 us -> 10.7 us  [weight_rows(): pl.pallas_call(functools.partial(weight_kernel, scale), grid_spec=pltpu.P...]
    all_to_all x1, starting transfers between devices: 6.03 us -> 4.51 us  [shards(): lax.all_to_all(pieces, 'z', split_axis=0, concat_axis=0, tiled=True)]
    pallas_call x2 -> x1, Pallas kernels: 3.5 us -> 2.24 us  [added(): pl.pallas_call(add_kernel, grid=(1,), in_specs=[first, second, whole, who...]
    unnamed x25 -> x21, local copies, waits for them, and re-layouts: 4.59 us -> 3.56 us
  transfers between devices with their start and end apart: 23 -> 23, of which waited for: 11 -> 8; matrix products, arithmetic and copies ran while one was open for 7% -> 8% of each run, Pallas kernels for 27% -> 28%
where the time goes in v2:
time: 146 us; the launch traced here: 145 us
  waiting for transfers between devices  47.9 us (33%)
  Pallas kernels  43.1 us (30%)
  starting transfers between devices  37.2 us (25%)
  local copies, waits for them, and re-layouts  11.2 us (8%)
  other arithmetic  5.06 us (3%)
    ppermute x4, waiting for transfers between devices, apart(): lax.ppermute(v, ('k', axis), [(n * core + i, n * core + j) for core, i, j...  29.3 us
    pallas_call x2, Pallas kernels, attention(): pl.pallas_call(attention_kernel, grid=(windows,), in_specs=[block] * 4 +...  14.8 us
    ppermute x14, starting transfers between devices, hop(): return lax.ppermute(v, axis, shifted(lax.axis_size(axis), by))  12.9 us
    pallas_call x2, Pallas kernels, weight_rows(): pl.pallas_call(functools.partial(weight_kernel, scale), grid_spec=pltpu.P...  10.7 us
    pallas_call x1, Pallas kernels, hidden_of(): pl.pallas_call(hidden_kernel, grid_spec=pltpu.PrefetchScalarGridSpec(num_...  10.3 us
    all_to_all x1, waiting for transfers between devices, shards(): cols = lax.all_to_all(blocks, DP, split_axis=0, concat_axis=0, tiled=True)  9.15 us
    all_to_all x1, starting transfers between devices, shards(): lax.all_to_all(outgoing.reshape(owners, cap, -1), CTX, split_axis=0, conc...  9.09 us
    all_to_all x1, starting transfers between devices, shards(): cols = lax.all_to_all(blocks, DP, split_axis=0, concat_axis=0, tiled=True)  5.99 us
  transfers between devices with their start and end apart: 23, of which 8 were waited for; matrix products, arithmetic and copies ran while one was open for 8% of the time, Pallas kernels for 28%

profile of v2, /device:TPU:2, one launch (start us, length us, event | category | flops | bytes accessed | tf_op | source)
XLA Modules:
  0.0 145.3 jit_solution(7333163093894455244)
XLA Ops:
  0.6 0.0 copy-start
  0.6 0.9 copy.20.own_ref
  1.5 1.0 copy-done.4
  2.5 0.8 pack.1
  3.4 1.1 act.1
  4.5 0.1 collective-permute-start
  4.6 3.0 %collective-permute-done = bf16[2560,256]{1,0:T(8,128)(2,1)S(1)} collective-permute-done((bf16[2560,256]{1,0:T(8,128)(2,1)S(1)}, bf16[2560,256]{1,0:T(8,128)(2,1)S(1)}, u32[]{:S(2)}, u32[]{:S(2)}) %collective-permute-start) | collective-permute-done | bytes 1310752 | tf_op jit(solution)/shard_map/ppermute | solution.py:374
  7.6 0.2 pad_maximum_fusion.own
  7.8 0.0 copy-start.9
  7.9 1.6 %collective-permute-start.6 = (bf16[2,2560,256]{2,1,0:T(8,128)(2,1)S(1)}, bf16[2,2560,256]{2,1,0:T(8,128)(2,1)}, u32[]{:S(2)}, u32[]{:S(2)}) collective-permute-start(bf16[2,2560,256]{2,1,0:T(8,128)(2,1)S(1)} %pad_maximum_fusion.own), channel_id=1, source_target_pairs={{0,64},{64,128},{128,192},{192,0},{32,224},{96,32},{160,96},{224,1... | collective-permute-start | bytes 7864328 | tf_op jit(solution)/shard_map/ppermute | solution.py:380
  9.4 1.6 %collective-permute-start.1 = (bf16[80,1792]{1,0:T(8,128)(2,1)S(1)}, bf16[80,1792]{1,0:T(8,128)(2,1)S(1)}, u32[]{:S(2)}, u32[]{:S(2)}) collective-permute-start(bf16[80,1792]{1,0:T(8,128)(2,1)S(1)} %copy-done.7), channel_id=1, source_target_pairs={{0,8},{8,16},{16,24},{24,0},{1,9},{9,17},{17,25},{25,1},{2,10},{10... | collective-permute-start | bytes 860168 | tf_op jit(solution)/shard_map/ppermute | solution.py:374
  11.0 2.9 %collective-permute-start.2 = (bf16[80,1792]{1,0:T(8,128)(2,1)S(1)}, bf16[80,1792]{1,0:T(8,128)(2,1)}, u32[]{:S(2)}, u32[]{:S(2)}) collective-permute-start(bf16[80,1792]{1,0:T(8,128)(2,1)S(1)} %copy-done.7), channel_id=1, source_target_pairs={{0,16},{8,24},{16,0},{24,8},{1,17},{9,25},{17,1},{25,9},{2,18},{10... | collective-permute-start | bytes 860168 | tf_op jit(solution)/shard_map/ppermute | solution.py:374
  13.9 1.3 collective-permute-start.3
  15.3 9.1 %all-to-all-start = ((bf16[32,8,1920]{2,1,0:T(8,128)(2,1)}), bf16[32,8,1920]{2,1,0:T(8,128)(2,1)}, u32[]{:S(2)}, u32[]{:S(2)}) async-start(bf16[32,8,1920]{2,1,0:T(8,128)(2,1)} %bitcast.32), calls=%async_computation | async-start | bytes 1966080 | tf_op jit(solution)/shard_map/all_to_all | solution.py:387
  24.4 0.1 broadcast_multiply_fusion.1
  24.5 0.1 copy.21
  24.6 1.2 fusion.8
  25.8 7.4 %attention.2 = (bf16[256,1280]{1,0:T(8,128)(2,1)}, bf16[256,1280]{1,0:T(8,128)(2,1)}, bf16[256,1280]{1,0:T(8,128)(2,1)}) custom-call(bf16[256,1280]{1,0:T(8,128)(2,1)} %q_ref.1, bf16[256,1280]{1,0:T(8,128)(2,1)} %k_ref.3, bf16[256,1280]{1,0:T(8,128)(2,1)} %v_ref.3, bf16[256,1280]{1,0:T(8,128)(2,1)} %g_ref.3, f32[256,40]{1,0:T(8,128)} %get-tuple-element.56.cos_ref, ...), custom_call_target="tpu_custom_call" | custom-call | flops 1677721600 | bytes 2949120 | tf_op jit(solution)/shard_map/attention/pallas_call | solution.py:342
  33.2 7.4 %attention.3 = (bf16[256,1280]{1,0:T(8,128)(2,1)}, bf16[256,1280]{1,0:T(8,128)(2,1)}, bf16[256,1280]{1,0:T(8,128)(2,1)}) custom-call(bf16[256,1280]{1,0:T(8,128)(2,1)} %q_ref.1, bf16[256,1280]{1,0:T(8,128)(2,1)} %k_ref.3, bf16[256,1280]{1,0:T(8,128)(2,1)} %v_ref.3, ...), custom_call_target="tpu_custom_call", output_to_operand_aliasing={{0}: (6, {}), {1}: (7, {}), {2}: (8, {})} | custom-call | flops 1677721600 | bytes 2949120 | tf_op jit(solution)/shard_map/attention/pallas_call | solution.py:342
  40.6 0.0 collective-permute-done.1
  40.6 2.5 %constant_dynamic-slice_fusion.1 = bf16[2,1280,256]{2,1,0:T(8,128)(2,1)} fusion(bf16[2,2560,256]{2,1,0:T(8,128)(2,1)} %collective-permute-done.6.mine, s32[]{:T(128)S(6)} %select_n.123), kind=kLoop, calls=%fused_computation.31 | loop fusion | bytes 2621444 | tf_op jit(solution)/shard_map/dynamic_slice | solution.py:405
  43.2 1.2 collective-permute-start.8
  44.4 5.7 %all-to-all-done = bf16[32,8,1920]{2,1,0:T(8,128)(2,1)} async-done(((bf16[32,8,1920]{2,1,0:T(8,128)(2,1)}), bf16[32,8,1920]{2,1,0:T(8,128)(2,1)}, u32[]{:S(2)}, u32[]{:S(2)}) %all-to-all-start) | async-done | bytes 983072 | tf_op jit(solution)/shard_map/all_to_all | solution.py:387
  50.1 3.0 %land.1 = (bf16[256,1792]{1,0:T(8,128)(2,1)}, bf16[8,224,256]{2,1,0:T(8,128)(2,1)}) custom-call(bf16[256,1920]{1,0:T(8,128)(2,1)} %bitcast.5.inc_ref), custom_call_target="tpu_custom_call" | custom-call | flops 234881024 | bytes 2752512 | tf_op jit(solution)/shard_map/land/pallas_call | solution.py:96
  53.1 6.0 %all-to-all-start.1 = ((bf16[8,224,256]{2,1,0:T(8,128)(2,1)}), bf16[8,224,256]{2,1,0:T(8,128)(2,1)S(1)}, u32[]{:S(2)}, u32[]{:S(2)}) async-start(bf16[8,224,256]{2,1,0:T(8,128)(2,1)} %get-tuple-element.42), calls=%async_computation.1 | async-start | bytes 1835008 | tf_op jit(solution)/shard_map/all_to_all | solution.py:409
  59.1 2.4 %pad_maximum_fusion.1.refs_0_ = bf16[4,80,1792]{2,1,0:T(8,128)(2,1)} fusion(bf16[1,80,1792]{2,1,0:T(8,128)(2,1)} %bitcast.9, bf16[1,80,1792]{2,1,0:T(8,128)(2,1)} %bitcast.8, bf16[1,80,1792]{2,1,0:T(8,128)(2,1)} %bitcast.35, bf16[1,80,1792]{2,1,0:T(8,128)(2,1)} %bitcast.34), kind=kLoop, calls=%fused_computation.1 | loop fusion | flops 1720320 | bytes 2293760 | tf_op jit(solution)/shard_map/stack | solution.py:431
  61.5 1.5 %collective-permute-start.4 = (bf16[4,80,1792]{2,1,0:T(8,128)(2,1)}, bf16[4,80,1792]{2,1,0:T(8,128)(2,1)}, u32[]{:S(2)}, u32[]{:S(2)}) collective-permute-start(bf16[4,80,1792]{2,1,0:T(8,128)(2,1)} %pad_maximum_fusion.1.refs_0_), channel_id=1, source_target_pairs={{0,1},{1,2},{2,3},{3,4},{4,5},{5,6},{6,7},{7,0},{32,39},{33,32},{3... | collective-permute-start | bytes 3440648 | tf_op jit(solution)/shard_map/ppermute | solution.py:381
  63.1 9.1 %all-to-all-done.1.cols_ref = bf16[8,224,256]{2,1,0:T(8,128)(2,1)S(1)} async-done(((bf16[8,224,256]{2,1,0:T(8,128)(2,1)}), bf16[8,224,256]{2,1,0:T(8,128)(2,1)S(1)}, u32[]{:S(2)}, u32[]{:S(2)}) %all-to-all-start.1) | async-done | bytes 917536 | tf_op jit(solution)/shard_map/all_to_all | solution.py:409
  72.2 6.7 %collective-permute-done.4.refs_1_ = bf16[4,80,1792]{2,1,0:T(8,128)(2,1)} collective-permute-done((bf16[4,80,1792]{2,1,0:T(8,128)(2,1)}, bf16[4,80,1792]{2,1,0:T(8,128)(2,1)}, u32[]{:S(2)}, u32[]{:S(2)}) %collective-permute-start.4) | collective-permute-done | bytes 1146912 | tf_op jit(solution)/shard_map/ppermute | solution.py:381
  78.9 0.3 collective-permute-start.5
  79.3 0.1 stack.117.idx_ref
  79.4 3.3 %weight.2 = f32[2,320,224]{2,1,0:T(8,128)S(1)} custom-call(s32[10]{0:T(128)S(1)} %stack.117.idx_ref, bf16[8,224,256]{2,1,0:T(8,128)(2,1)S(1)} %all-to-all-done.1.cols_ref, bf16[2,2560,256]{2,1,0:T(8,128)(2,1)S(1)} %pad_maximum_fusion.own, bf16[2,2560,256]{2,1,0:T(8,128)(2,1)} %collective-permute-done.6.mine, ...), custom_call_target="tpu_custom_call" | custom-call | flops 587202560 | bytes 2621440 | tf_op jit(solution)/shard_map/weight/pallas_call | solution.py:220
  82.7 0.9 slice_bitcast_fusion
  83.6 0.6 collective-permute-start.10
  84.2 2.6 %collective-permute-start.11 = (f32[320,224]{1,0:T(8,128)}, f32[320,224]{1,0:T(8,128)}, u32[]{:S(2)}, u32[]{:S(2)}) collective-permute-start(f32[320,224]{1,0:T(8,128)} %get-tuple-element.53), channel_id=1, source_target_pairs={{0,24},{8,0},{16,8},{24,16},{1,25},{9,1},{17,9},{25,17},{2,26},{10... | collective-permute-start | bytes 860168 | tf_op jit(solution)/shard_map/ppermute | solution.py:374
  86.8 0.1 stack.127.idx_ref
  86.9 7.4 %weight.3 = (f32[2,320,224]{2,1,0:T(8,128)}, f32[2,320,224]{2,1,0:T(8,128)}, f32[2,320,224]{2,1,0:T(8,128)S(1)}) custom-call(s32[14]{0:T(128)S(1)} %stack.127.idx_ref, bf16[8,224,256]{2,1,0:T(8,128)(2,1)S(1)} %all-to-all-done.1.cols_ref, bf16[2,2560,256]{2,1,0:T(8,128)(2,1)S(1)} %pad_maximum_fusion.own, bf16[2,2560,256]{2,1,0:T(8,128)(2,1)} %collective-permute-done.6.mine, ...), custom_call_target="tpu_custom_call" | custom-call | flops 1761607680 | bytes 7864320 | tf_op jit(solution)/shard_map/weight/pallas_call | solution.py:220
  94.3 0.8 copy-done.2
  95.2 1.2 collective-permute-done.5.refs_2_
  96.3 2.2 %add.213 = (f32[2,320,224]{2,1,0:T(8,128)}, f32[2,320,224]{2,1,0:T(8,128)}) custom-call(f32[2,320,224]{2,1,0:T(8,128)} %get-tuple-element.48.above_ref, f32[2,320,224]{2,1,0:T(8,128)} %get-tuple-element.49.below_ref, f32[320,224]{1,0:T(8,128)} %collective-permute-done.10.low_ref, ...), custom_call_target="tpu_custom_call", output_to_operand_aliasing={{0}: (0, {}), {1}: (1, {})} | custom-call | flops 143360 | bytes 1720320 | tf_op jit(solution)/shard_map/add/pallas_call | solution.py:245
  98.6 3.2 %collective-permute-start.19 = (f32[2,320,224]{2,1,0:T(8,128)}, f32[2,320,224]{2,1,0:T(8,128)S(1)}, u32[]{:S(2)}, u32[]{:S(2)}) collective-permute-start(f32[2,320,224]{2,1,0:T(8,128)} %get-tuple-element.51), channel_id=1, source_target_pairs={{0,24},{8,0},{16,8},{24,16},{1,25},{9,1},{17,9},{25,17},{2,26},{10... | collective-permute-start | bytes 1720328 | tf_op jit(solution)/shard_map/ppermute | solution.py:374
  101.8 11.9 %collective-permute-done.12.refs_3_ = bf16[4,80,1792]{2,1,0:T(8,128)(2,1)} collective-permute-done((bf16[4,80,1792]{2,1,0:T(8,128)(2,1)}, bf16[4,80,1792]{2,1,0:T(8,128)(2,1)}, u32[]{:S(2)}, u32[]{:S(2)}) %collective-permute-start.12) | collective-permute-done | bytes 1146912 | tf_op jit(solution)/shard_map/ppermute | solution.py:381
  113.7 1.9 %constant_dynamic-slice_fusion = bf16[2,80,1792]{2,1,0:T(8,128)(2,1)} fusion(bf16[4,80,1792]{2,1,0:T(8,128)(2,1)} %collective-permute-done.12.refs_3_, s32[]{:T(128)S(6)} %select_n.127), kind=kLoop, calls=%fused_computation.30 | loop fusion | bytes 1146884 | tf_op jit(solution)/shard_map/dynamic_slice | solution.py:435
  115.6 0.5 collective-permute-start.15
  116.1 0.0 collective-permute-start.16
  116.1 1.0 add_add_fusion
  117.1 4.5 %all-to-all-start.2 = ((f32[8,80,224]{2,1,0:T(8,128)}), f32[8,80,224]{2,1,0:T(8,128)S(1)}, u32[]{:S(2)}, u32[]{:S(2)}) async-start(f32[8,80,224]{2,1,0:T(8,128)} %bitcast.28), calls=%async_computation.2 | async-start | bytes 1310720 | tf_op jit(solution)/shard_map/all_to_all | solution.py:450
  121.7 9.6 %collective-permute-done.13.refs_4_ = bf16[2,80,1792]{2,1,0:T(8,128)(2,1)} collective-permute-done((bf16[2,80,1792]{2,1,0:T(8,128)(2,1)}, bf16[2,80,1792]{2,1,0:T(8,128)(2,1)}, u32[]{:S(2)}, u32[]{:S(2)}) %collective-permute-start.13) | collective-permute-done | bytes 573472 | tf_op jit(solution)/shard_map/ppermute | solution.py:381
  131.3 0.1 broadcast_in_dim.76
  131.3 0.1 broadcast_in_dim.77
  131.4 0.1 broadcast_in_dim.86
  131.5 0.1 broadcast_in_dim.87
  131.6 0.1 broadcast_in_dim.80
  131.6 0.1 broadcast_in_dim.81
  131.8 0.1 broadcast_in_dim.79
  131.9 0.1 broadcast_in_dim.83
  132.0 0.1 add.161
  132.1 0.1 broadcast_in_dim.75
  132.2 0.5 fusion.2.at_ref
  132.7 0.7 collective-permute-done.17.refs_8_
  133.4 0.3 copy-done.5
  133.7 0.5 copy-done.6
  134.3 10.3 %hidden.1 = bf16[256,2560]{1,0:T(8,128)(2,1)} custom-call(s32[32]{0:T(128)} %fusion.2.at_ref, bf16[256,1792]{1,0:T(8,128)(2,1)} %get-tuple-element.39.slot_ref, bf16[256,2560]{1,0:T(8,128)(2,1)} %pre_ref.2, bf16[4,80,1792]{2,1,0:T(8,128)(2,1)} %pad_maximum_fusion.1.refs_0_, bf16[4,80,1792]{2,1,0:T(8,128)(2,1)} %collective-permute-done.4.refs_1_, ...), custom_call_target="tpu_custom_call" | custom-call | flops 2348810240 | bytes 11796480 | tf_op jit(solution)/shard_map/hidden/pallas_call | solution.py:160
  144.6 0.7 reduce_sum.9
  (47 shorter events, 0.2 us)
Async XLA Ops:
  0.6 2.7 %copy-start = (bf16[256,2560]{1,0:T(8,128)(2,1)S(1)}, bf16[256,2560]{1,0:T(8,128)(2,1)}, u32[]{:S(2)}) copy-start(bf16[256,2560]{1,0:T(8,128)(2,1)} %pre_ref.2) | copy-start | bytes 3932164
  1.5 1.0 copy-start.4
  3.4 4.2 %copy-start.1 = (bf16[256,1920]{1,0:T(8,128)(2,1)}, bf16[256,1920]{1,0:T(8,128)(2,1)S(1)}, u32[]{:S(2)}) copy-start(bf16[256,1920]{1,0:T(8,128)(2,1)S(1)} %pack.1) | copy-start | bytes 2949124
  4.5 3.1 %collective-permute-start = (bf16[2560,256]{1,0:T(8,128)(2,1)S(1)}, bf16[2560,256]{1,0:T(8,128)(2,1)S(1)}, u32[]{:S(2)}, u32[]{:S(2)}) collective-permute-start(bf16[2560,256]{1,0:T(8,128)(2,1)S(1)} %act.1), channel_id=1, source_target_pairs={{0,32},{32,0},{1,33},{33,1},{2,34},{34,2},{3,35},{35,3},{4,36},{36... | collective-permute-start | bytes 3932168 | tf_op jit(solution)/shard_map/ppermute | solution.py:374
  7.6 1.8 %copy-start.7 = (bf16[80,1792]{1,0:T(8,128)(2,1)S(1)}, bf16[80,1792]{1,0:T(8,128)(2,1)}, u32[]{:S(2)}) copy-start(bf16[80,1792]{1,0:T(8,128)(2,1)} %param.12) | copy-start | bytes 860164
  7.8 16.5 %copy-start.9 = (s32[2,256]{1,0:T(2,128)S(1)}, s32[2,256]{1,0:T(2,128)}, u32[]{:S(2)}) copy-start(s32[2,256]{1,0:T(2,128)} %param.17) | copy-start | bytes 6148
  7.9 32.8 %collective-permute-start.6 = (bf16[2,2560,256]{2,1,0:T(8,128)(2,1)S(1)}, bf16[2,2560,256]{2,1,0:T(8,128)(2,1)}, u32[]{:S(2)}, u32[]{:S(2)}) collective-permute-start(bf16[2,2560,256]{2,1,0:T(8,128)(2,1)S(1)} %pad_maximum_fusion.own), channel_id=1, source_target_pairs={{0,64},{64,128},{128,192},{192,0},{32,224},{96,32},{160,96},{224,1... | collective-permute-start | bytes 7864328 | tf_op jit(solution)/shard_map/ppermute | solution.py:380
  9.4 31.2 %collective-permute-start.1 = (bf16[80,1792]{1,0:T(8,128)(2,1)S(1)}, bf16[80,1792]{1,0:T(8,128)(2,1)S(1)}, u32[]{:S(2)}, u32[]{:S(2)}) collective-permute-start(bf16[80,1792]{1,0:T(8,128)(2,1)S(1)} %copy-done.7), channel_id=1, source_target_pairs={{0,8},{8,16},{16,24},{24,0},{1,9},{9,17},{17,25},{25,1},{2,10},{10... | collective-permute-start | bytes 860168 | tf_op jit(solution)/shard_map/ppermute | solution.py:374
  11.0 29.6 %collective-permute-start.2 = (bf16[80,1792]{1,0:T(8,128)(2,1)S(1)}, bf16[80,1792]{1,0:T(8,128)(2,1)}, u32[]{:S(2)}, u32[]{:S(2)}) collective-permute-start(bf16[80,1792]{1,0:T(8,128)(2,1)S(1)} %copy-done.7), channel_id=1, source_target_pairs={{0,16},{8,24},{16,0},{24,8},{1,17},{9,25},{17,1},{25,9},{2,18},{10... | collective-permute-start | bytes 860168 | tf_op jit(solution)/shard_map/ppermute | solution.py:374
  13.9 26.7 %collective-permute-start.3 = (bf16[80,1792]{1,0:T(8,128)(2,1)S(1)}, bf16[80,1792]{1,0:T(8,128)(2,1)}, u32[]{:S(2)}, u32[]{:S(2)}) collective-permute-start(bf16[80,1792]{1,0:T(8,128)(2,1)S(1)} %copy-done.7), channel_id=1, source_target_pairs={{0,24},{8,0},{16,8},{24,16},{1,25},{9,1},{17,9},{25,17},{2,26},{10... | collective-permute-start | bytes 860168 | tf_op jit(solution)/shard_map/ppermute | solution.py:374
  15.3 34.8 %all-to-all-start = ((bf16[32,8,1920]{2,1,0:T(8,128)(2,1)}), bf16[32,8,1920]{2,1,0:T(8,128)(2,1)}, u32[]{:S(2)}, u32[]{:S(2)}) async-start(bf16[32,8,1920]{2,1,0:T(8,128)(2,1)} %bitcast.32), calls=%async_computation | async-start | bytes 1966080 | tf_op jit(solution)/shard_map/all_to_all | solution.py:387
  40.6 2.6 %copy-start.8 = (bf16[80,1792]{1,0:T(8,128)(2,1)}, bf16[80,1792]{1,0:T(8,128)(2,1)S(1)}, u32[]{:S(2)}) copy-start(bf16[80,1792]{1,0:T(8,128)(2,1)S(1)} %collective-permute-done.1) | copy-start | bytes 860164
  43.2 29.1 %collective-permute-start.8 = (bf16[2,1280,256]{2,1,0:T(8,128)(2,1)}, bf16[2,1280,256]{2,1,0:T(8,128)(2,1)}, u32[]{:S(2)}, u32[]{:S(2)}) collective-permute-start(bf16[2,1280,256]{2,1,0:T(8,128)(2,1)} %constant_dynamic-slice_fusion.1), channel_id=1, source_target_pairs={{0,64},{64,128},{128,192},{192,0},{32,224},{96,32},{160,96},{224,1... | collective-permute-start | bytes 3932168 | tf_op jit(solution)/shard_map/ppermute | solution.py:380
  44.4 35.0 %collective-permute-start.7 = (bf16[2,2560,256]{2,1,0:T(8,128)(2,1)}, bf16[2,2560,256]{2,1,0:T(8,128)(2,1)}, u32[]{:S(2)}, u32[]{:S(2)}) collective-permute-start(bf16[2,2560,256]{2,1,0:T(8,128)(2,1)} %collective-permute-done.6.mine), channel_id=1, source_target_pairs={{0,32},{32,0},{1,33},{33,1},{2,34},{34,2},{3,35},{35,3},{4,36},{36... | collective-permute-start | bytes 7864328 | tf_op jit(solution)/shard_map/ppermute | solution.py:374
  53.1 19.1 %all-to-all-start.1 = ((bf16[8,224,256]{2,1,0:T(8,128)(2,1)}), bf16[8,224,256]{2,1,0:T(8,128)(2,1)S(1)}, u32[]{:S(2)}, u32[]{:S(2)}) async-start(bf16[8,224,256]{2,1,0:T(8,128)(2,1)} %get-tuple-element.42), calls=%async_computation.1 | async-start | bytes 1835008 | tf_op jit(solution)/shard_map/all_to_all | solution.py:409
  61.5 17.4 %collective-permute-start.4 = (bf16[4,80,1792]{2,1,0:T(8,128)(2,1)}, bf16[4,80,1792]{2,1,0:T(8,128)(2,1)}, u32[]{:S(2)}, u32[]{:S(2)}) collective-permute-start(bf16[4,80,1792]{2,1,0:T(8,128)(2,1)} %pad_maximum_fusion.1.refs_0_), channel_id=1, source_target_pairs={{0,1},{1,2},{2,3},{3,4},{4,5},{5,6},{6,7},{7,0},{32,39},{33,32},{3... | collective-permute-start | bytes 3440648 | tf_op jit(solution)/shard_map/ppermute | solution.py:381
  72.2 7.1 %collective-permute-start.9 = (bf16[2,1280,256]{2,1,0:T(8,128)(2,1)}, bf16[2,1280,256]{2,1,0:T(8,128)(2,1)}, u32[]{:S(2)}, u32[]{:S(2)}) collective-permute-start(bf16[2,1280,256]{2,1,0:T(8,128)(2,1)} %collective-permute-done.8.mine_half), channel_id=1, source_target_pairs={{0,32},{32,0},{1,33},{33,1},{2,34},{34,2},{3,35},{35,3},{4,36},{36... | collective-permute-start | bytes 3932168 | tf_op jit(solution)/shard_map/ppermute | solution.py:374
  78.9 17.4 %collective-permute-start.5 = (bf16[4,80,1792]{2,1,0:T(8,128)(2,1)}, bf16[4,80,1792]{2,1,0:T(8,128)(2,1)}, u32[]{:S(2)}, u32[]{:S(2)}) collective-permute-start(bf16[4,80,1792]{2,1,0:T(8,128)(2,1)} %collective-permute-done.4.refs_1_), channel_id=1, source_target_pairs={{0,1},{1,2},{2,3},{3,4},{4,5},{5,6},{6,7},{7,0},{32,39},{33,32},{3... | collective-permute-start | bytes 3440648 | tf_op jit(solution)/shard_map/ppermute | solution.py:381
  83.6 12.7 %collective-permute-start.10 = (f32[320,224]{1,0:T(8,128)}, f32[320,224]{1,0:T(8,128)}, u32[]{:S(2)}, u32[]{:S(2)}) collective-permute-start(f32[320,224]{1,0:T(8,128)} %get-tuple-element.54), channel_id=1, source_target_pairs={{0,8},{8,16},{16,24},{24,0},{1,9},{9,17},{17,25},{25,1},{2,10},{10... | collective-permute-start | bytes 860168 | tf_op jit(solution)/shard_map/ppermute | solution.py:374
  84.2 12.1 %collective-permute-start.11 = (f32[320,224]{1,0:T(8,128)}, f32[320,224]{1,0:T(8,128)}, u32[]{:S(2)}, u32[]{:S(2)}) collective-permute-start(f32[320,224]{1,0:T(8,128)} %get-tuple-element.53), channel_id=1, source_target_pairs={{0,24},{8,0},{16,8},{24,16},{1,25},{9,1},{17,9},{25,17},{2,26},{10... | collective-permute-start | bytes 860168 | tf_op jit(solution)/shard_map/ppermute | solution.py:374
  94.3 0.8 copy-start.2
  96.3 17.4 %collective-permute-start.12 = (bf16[4,80,1792]{2,1,0:T(8,128)(2,1)}, bf16[4,80,1792]{2,1,0:T(8,128)(2,1)}, u32[]{:S(2)}, u32[]{:S(2)}) collective-permute-start(bf16[4,80,1792]{2,1,0:T(8,128)(2,1)} %collective-permute-done.5.refs_2_), channel_id=1, source_target_pairs={{0,1},{1,2},{2,3},{3,4},{4,5},{5,6},{6,7},{7,0},{32,39},{33,32},{3... | collective-permute-start | bytes 3440648 | tf_op jit(solution)/shard_map/ppermute | solution.py:381
  96.3 19.8 %copy-start.3 = (f32[2,320,224]{2,1,0:T(8,128)S(1)}, f32[2,320,224]{2,1,0:T(8,128)}, u32[]{:S(2)}) copy-start(f32[2,320,224]{2,1,0:T(8,128)} %copy-done.2) | copy-start | bytes 1720324
  98.6 17.5 %collective-permute-start.18 = (f32[2,320,224]{2,1,0:T(8,128)}, f32[2,320,224]{2,1,0:T(8,128)S(1)}, u32[]{:S(2)}, u32[]{:S(2)}) collective-permute-start(f32[2,320,224]{2,1,0:T(8,128)} %get-tuple-element.50), channel_id=1, source_target_pairs={{0,8},{8,16},{16,24},{24,0},{1,9},{9,17},{17,25},{25,1},{2,10},{10... | collective-permute-start | bytes 1720328 | tf_op jit(solution)/shard_map/ppermute | solution.py:374
  98.6 17.5 %collective-permute-start.19 = (f32[2,320,224]{2,1,0:T(8,128)}, f32[2,320,224]{2,1,0:T(8,128)S(1)}, u32[]{:S(2)}, u32[]{:S(2)}) collective-permute-start(f32[2,320,224]{2,1,0:T(8,128)} %get-tuple-element.51), channel_id=1, source_target_pairs={{0,24},{8,0},{16,8},{24,16},{1,25},{9,1},{17,9},{25,17},{2,26},{10... | collective-permute-start | bytes 1720328 | tf_op jit(solution)/shard_map/ppermute | solution.py:374
  115.6 15.7 %collective-permute-start.13 = (bf16[2,80,1792]{2,1,0:T(8,128)(2,1)}, bf16[2,80,1792]{2,1,0:T(8,128)(2,1)}, u32[]{:S(2)}, u32[]{:S(2)}) collective-permute-start(bf16[2,80,1792]{2,1,0:T(8,128)(2,1)} %constant_dynamic-slice_fusion), channel_id=1, source_target_pairs={{0,1},{1,2},{2,3},{3,4},{4,5},{5,6},{6,7},{7,0},{32,39},{33,32},{3... | collective-permute-start | bytes 1720328 | tf_op jit(solution)/shard_map/ppermute | solution.py:381
  115.6 17.1 %collective-permute-start.14 = (bf16[4,80,1792]{2,1,0:T(8,128)(2,1)}, bf16[4,80,1792]{2,1,0:T(8,128)(2,1)S(1)}, u32[]{:S(2)}, u32[]{:S(2)}) collective-permute-start(bf16[4,80,1792]{2,1,0:T(8,128)(2,1)} %collective-permute-done.4.refs_1_), channel_id=1, source_target_pairs={{0,32},{32,0},{1,33},{33,1},{2,34},{34,2},{3,35},{35,3},{4,36},{36... | collective-permute-start | bytes 3440648 | tf_op jit(solution)/shard_map/ppermute | solution.py:374
  115.6 17.1 %collective-permute-start.15 = (bf16[4,80,1792]{2,1,0:T(8,128)(2,1)}, bf16[4,80,1792]{2,1,0:T(8,128)(2,1)}, u32[]{:S(2)}, u32[]{:S(2)}) collective-permute-start(bf16[4,80,1792]{2,1,0:T(8,128)(2,1)} %collective-permute-done.5.refs_2_), channel_id=1, source_target_pairs={{0,32},{32,0},{1,33},{33,1},{2,34},{34,2},{3,35},{35,3},{4,36},{36... | collective-permute-start | bytes 3440648 | tf_op jit(solution)/shard_map/ppermute | solution.py:374
  116.1 17.3 %collective-permute-start.16 = (bf16[4,80,1792]{2,1,0:T(8,128)(2,1)}, bf16[4,80,1792]{2,1,0:T(8,128)(2,1)}, u32[]{:S(2)}, u32[]{:S(2)}) collective-permute-start(bf16[4,80,1792]{2,1,0:T(8,128)(2,1)} %collective-permute-done.12.refs_3_), channel_id=1, source_target_pairs={{0,32},{32,0},{1,33},{33,1},{2,34},{34,2},{3,35},{35,3},{4,36},{36... | collective-permute-start | bytes 3440648 | tf_op jit(solution)/shard_map/ppermute | solution.py:374
  117.1 27.4 %all-to-all-start.2 = ((f32[8,80,224]{2,1,0:T(8,128)}), f32[8,80,224]{2,1,0:T(8,128)S(1)}, u32[]{:S(2)}, u32[]{:S(2)}) async-start(f32[8,80,224]{2,1,0:T(8,128)} %bitcast.28), calls=%async_computation.2 | async-start | bytes 1310720 | tf_op jit(solution)/shard_map/all_to_all | solution.py:450
  131.2 2.2 %collective-permute-start.17 = (bf16[2,80,1792]{2,1,0:T(8,128)(2,1)}, bf16[2,80,1792]{2,1,0:T(8,128)(2,1)S(1)}, u32[]{:S(2)}, u32[]{:S(2)}) collective-permute-start(bf16[2,80,1792]{2,1,0:T(8,128)(2,1)} %collective-permute-done.13.refs_4_), channel_id=1, source_target_pairs={{0,32},{32,0},{1,33},{33,1},{2,34},{34,2},{3,35},{35,3},{4,36},{36... | collective-permute-start | bytes 1720328 | tf_op jit(solution)/shard_map/ppermute | solution.py:374
  132.7 1.0 copy-start.5
  133.4 0.8 copy-start.6
